TPU v7x, 512 devices: a whole 4x8x8 slice. The times are simulated.
512 devices in a mesh: pair: 32 (over x, z), aux: 16 (over y, core).
Axes of the slice: x: 4, y: 8, z: 8, core: 2. Of those that a mesh axis runs over, the one named last changes fastest.
Arguments:
- amps: bfloat16 [4096, 128, 128], P(('pair', 'aux')), may hold values from -6 to 6
- rotation: bfloat16 [4096, 128, 128], P(('pair', 'aux')), may hold values from -0.5 to 0.5
- intersections: bfloat16 [4096, 4, 128, 128], P(('pair', 'aux')), may hold values from -0.5 to 0.5
- energies: float32 [4096, 128], P(('pair', 'aux')), may hold values from 0.25 to 2
- domains: int32 [4096, 2], P(('pair', 'aux')), may hold values from 0 to 31
- owners: int32 [4096, 4], P(('pair', 'aux')), may hold values from 0 to 31, all different within a row; in each aligned block of 8 rows (0 to 7, 8 to 15, ...) at most 2 rows name the same one
- slots: int32 [4096, 4], P(('pair', 'aux')), may hold values from 0 to 7
- tiles: int32 [4096], P(('pair', 'aux')), may hold values from 0 to 31
- blocks: bfloat16 [32, 512, 128], P('aux'), may hold values from -3 to 3
- coeffs: bfloat16 [32, 128, 4096], P('pair', None, 'aux'), may hold values from -0.5 to 0.5
Outputs:
- new_amps: bfloat16 [4096, 128, 128], P(('pair', 'aux'))
- density: float32 [32, 128, 4096], P('pair', None, 'aux')
Inputs may be any that keep to these rules, and one draw needn't show every extreme that they name: Each row names distinct owners; among the rows of one device no owner is named by more than 2 entries, a bound that some block reaches.
All inputs are finite; a program needn't handle non-finite values.
Results may differ from a plain program's by a relative error of at most 0.014.
Values may be sent and summed in bfloat16 or wider, within the bound.
No kernel may reach another device: no remote copies, remote signals or barrier semaphores. Data moves between devices by JAX's collectives and lax.ppermute only.
A program may use at most 64 MiB of HBM per device.

v0:
```python
import jax
import jax.numpy as jnp
from jax import lax
from jax.experimental import pallas as pl
from jax.experimental.pallas import tpu as pltpu
from jax.sharding import Mesh
from jax.sharding import PartitionSpec as P


F32 = jnp.float32
BF16 = jnp.bfloat16
CAP = 2
PAIR = ("x", "z")
AUX = ("y", "core")
FINE = (4, 8, 8, 2)
SUB = 8
CORES = 2
VMEM = pl.BlockSpec(memory_space=pltpu.VMEM)
SMEM = pl.BlockSpec(memory_space=pltpu.SMEM)
HBM = pl.BlockSpec(memory_space=pltpu.HBM)
PLACE = (0, 4, 2, 7, 1, 5, 3, 6)


def mm(a, b, ca=1, cb=0):
    return lax.dot_general(a, b, (((ca,), (cb,)), ((), ())), preferred_element_type=F32)


def call(kernel, out_shape, in_specs, out_specs, args, flops, bytes_accessed, scratch=(), mib=12):
    return pl.pallas_call(
        kernel,
        out_shape=out_shape,
        in_specs=in_specs,
        out_specs=out_specs,
        scratch_shapes=list(scratch),
        compiler_params=pltpu.CompilerParams(vmem_limit_bytes=mib << 20),
        cost_estimate=pl.CostEstimate(
            flops=flops, bytes_accessed=bytes_accessed, transcendentals=0
        ),
    )(*args)


def plan_kernel(owner_ref, slot_ref, want_ref, pos_ref, count):
    neighbours, pairs = owner_ref.shape
    rows, width = want_ref.shape

    @pl.loop(0, rows)
    def _(o):
        for i in range(width):
            want_ref[o, i] = 0
        for i in range(width // CAP):
            count[o * (width // CAP) + i] = 0

    @pl.loop(0, pairs)
    def _(p):
        for n in range(neighbours):
            o = owner_ref[n, p]
            r = count[o]
            count[o] = r + 1
            at = o * CAP + r
            pos_ref[p * neighbours + n] = at
            want_ref[at // width, lax.rem(at, width)] = slot_ref[n, p] + 1


def push_kernel(pos_ref, amps_ref, inter_ref, send_ref, *scratch):
    amps_buf, inter_buf, block_buf, sems, amps_sems, inter_sems = scratch
    pairs, neighbours, v, _ = inter_ref.shape
    step = 2

    def get(p):
        return (
            pltpu.make_async_copy(amps_ref.at[p], amps_buf.at[p], amps_sems.at[p]),
            pltpu.make_async_copy(inter_ref.at[p], inter_buf.at[p], inter_sems.at[p]),
        )

    def put(e):
        return pltpu.make_async_copy(block_buf.at[e], send_ref.at[pos_ref[e]], sems.at[e])

    def put_all(g):
        for i in range(step * neighbours):
            put(g * step * neighbours + i).start()

    for p in range(pairs):
        for copy in get(p):
            copy.start()

    @pl.loop(0, pairs // step)
    def _(g):
        for i in range(step):
            for copy in get(g * step + i):
                copy.wait()
        overs = [[inter_buf[g * step + i, n] for n in range(neighbours)] for i in range(step)]
        halves = [
            mm(jnp.concatenate(overs[i], axis=1), amps_buf[g * step + i], 0, 0).astype(BF16)
            for i in range(step)
        ]
        for i in range(step):
            for n in range(neighbours):
                block = mm(halves[i][n * v : (n + 1) * v, :], overs[i][n]).astype(BF16)
                block_buf[(g * step + i) * neighbours + n] = block

        @pl.when(g > 0)
        def _():
            put_all(g - 1)

    put_all(pairs // step - 1)

    @pl.loop(0, pairs * neighbours)
    def _(e):
        put(e).wait()


def reply_kernel(want_ref, held_ref, out_ref):
    rows, width = want_ref.shape
    per = held_ref.shape[0] // (width // CAP)

    @pl.loop(0, rows)
    def _(d):
        for i in range(width):
            out_ref[d, i] = held_ref[i // CAP * per + jnp.maximum(want_ref[d, i] - 1, 0)]


def sum_kernel(want_ref, recv_ref, out_ref, total):
    rows, width = want_ref.shape
    per = total.shape[0]

    @pl.loop(0, width // CAP)
    def _(o):
        total[...] = jnp.zeros(total.shape, F32)
        for d in range(rows):
            for r in range(CAP):
                s = want_ref[d, o * CAP + r]

                @pl.when(s > 0)
                def _():
                    total[s - 1] += recv_ref[d, o * CAP + r].astype(F32)

        out_ref[pl.ds(o * per, per)] = total[...].astype(BF16)


def denominator(energy_ref, p):
    v = energy_ref.shape[1]
    across = jnp.broadcast_to(energy_ref[pl.ds(p, 1), :], (v, v))
    return across.T + across


def integral_kernel(
    domain_ref, me_ref, own_ref, other_ref, rot_ref, amps_ref, energy_ref, out_ref
):
    pairs = rot_ref.shape[0]
    per = own_ref.shape[0] // len(PLACE)
    chip = me_ref[0] // CORES
    core = lax.rem(me_ref[0], CORES)

    @pl.loop(0, pairs)
    def _(p):
        rot = rot_ref[p]

        def block(side):
            d = domain_ref[side, p]
            device = d // per
            back = lax.rem(chip - device // CORES + len(PLACE), len(PLACE))
            place = jnp.int32(PLACE[0])
            for k in range(1, len(PLACE)):
                place = jnp.where(back == k, PLACE[k], place)
            at = place * per + lax.rem(d, per)
            same = (lax.rem(device, CORES) == core).astype(jnp.int32)
            pick = jnp.full((1, 1), same) > 0
            return jnp.where(pick, own_ref[at], other_ref[at])

        left = mm(rot, block(0), 0, 1).astype(BF16)
        right = mm(block(1), rot).astype(BF16)
        amp = amps_ref[p].astype(F32)
        out_ref[p] = mm(left, right) + denominator(energy_ref, p) * amp


def pull_kernel(pos_ref, arrived_ref, inter_ref, out_ref, part, sems):
    pairs, neighbours, _, _ = inter_ref.shape
    step = 4

    def get(e):
        return pltpu.make_async_copy(arrived_ref.at[pos_ref[e]], part.at[e], sems.at[e])

    @pl.loop(0, pairs * neighbours)
    def _(e):
        get(e).start()

    @pl.loop(0, pairs // step)
    def _(g):
        at = [g * step + i for i in range(step)]
        for p in at:
            for n in range(neighbours):
                get(p * neighbours + n).wait()
        halves = [
            [
                mm(inter_ref[p, n], part[p * neighbours + n]).astype(BF16)
                for n in range(neighbours)
            ]
            for p in at
        ]
        for p, half in zip(at, halves):
            out_ref[p] = mm(
                jnp.concatenate(half, axis=1),
                jnp.concatenate([inter_ref[p, n] for n in range(neighbours)], axis=1),
                1,
                1,
            )


def update_kernel(
    incoming_ref, amps_ref, rot_ref, energy_ref, base_ref, pulled_ref, note_ref, new_ref, out_ref
):
    pairs, v, _ = amps_ref.shape
    slabs = out_ref.shape[0]
    step = 4

    for r in range(slabs):
        out_ref[r, pairs] = note_ref[...]

    @pl.loop(0, pairs // step)
    def _(g):
        at = [g * step + i for i in range(step)]
        news = []
        for p in at:
            residual = base_ref[p] - pulled_ref[p] - incoming_ref[p].astype(F32)
            amp = amps_ref[p].astype(F32)
            news.append((amp - residual / (denominator(energy_ref, p) + 1.0)).astype(BF16))
        densities = [(mm(new, new, 1, 1) * (1.0 / v)).astype(BF16) for new in news]
        rots = [mm(rot_ref[p], d).astype(BF16) for p, d in zip(at, densities)]
        for p, new, rotated in zip(at, news, rots):
            new_ref[p] = new
            tile = mm(rotated, rot_ref[p], 1, 1).astype(BF16)
            for r in range(slabs):
                out_ref[r, p] = tile[r * SUB : (r + 1) * SUB, :]


def slab_kernel(recv_ref, out_ref, wide, total):
    sources, blocks, _, _ = recv_ref.shape
    pairs = blocks - 1
    count = out_ref.shape[0]
    wide[...] = recv_ref[:, :pairs].astype(F32).reshape(wide.shape)
    ids = jnp.sum(recv_ref[:, pairs].astype(F32), axis=0)[0:1, :]
    which = lax.broadcasted_iota(jnp.int32, (count, sources * pairs), 0).astype(F32)
    hot = (which == ids).astype(F32).astype(BF16)
    for s in range(SUB):
        rows = wide[pl.ds(s, sources * pairs, stride=SUB), :].astype(BF16)
        total[:, s, :] = mm(hot, rows)
    out_ref[...] = total[...].astype(BF16)


def local(amps, rotation, intersections, energies, domains, owners, slots, tiles, blocks, coeffs):
    pairs, v, _ = amps.shape
    neighbours = owners.shape[1]
    group = lax.axis_size(PAIR)
    ring = lax.axis_size(AUX)
    chips = ring // CORES
    entries = pairs * neighbours
    cube = v * v
    me = lax.axis_index(AUX).astype(jnp.int32)

    assert chips == len(PLACE)

    def shift(value, k):
        return lax.ppermute(value, "y", [(j, (j + k) % chips) for j in range(chips)])

    opposite = shift(blocks, 4)
    above, below = shift(blocks, 2), shift(blocks, -2)
    column = lax.all_gather(amps, "z", axis=0, tiled=True)
    across = lax.axis_size("x")
    width = CAP * group // across
    want, position = call(
        plan_kernel,
        (
            jax.ShapeDtypeStruct((across, width), jnp.int32),
            jax.ShapeDtypeStruct((entries,), jnp.int32),
        ),
        [SMEM, SMEM],
        (SMEM, SMEM),
        (owners.T, slots.T),
        0,
        1024,
        [pltpu.SMEM((group,), jnp.int32)],
    )
    asked = lax.all_to_all(want, "x", 0, 0, tiled=True)
    send = call(
        push_kernel,
        jax.ShapeDtypeStruct((group * CAP, v, v), BF16),
        [SMEM, HBM, HBM],
        HBM,
        (position, amps, intersections),
        4 * entries * cube * v,
        2 * cube * (pairs + entries + group * CAP),
        [
            pltpu.VMEM((pairs, v, v), BF16),
            pltpu.VMEM((pairs, neighbours, v, v), BF16),
            pltpu.VMEM((entries, v, v), BF16),
            pltpu.SemaphoreType.DMA((entries,)),
            pltpu.SemaphoreType.DMA((pairs,)),
            pltpu.SemaphoreType.DMA((pairs,)),
        ],
        58,
    )
    send, asked = lax.optimization_barrier((send, asked))
    recv = lax.all_to_all(send.reshape(across, width, v, v), "x", 0, 0, tiled=True)
    recv, opposite = lax.optimization_barrier((recv, opposite))
    sums = call(
        sum_kernel,
        jax.ShapeDtypeStruct((group // across * pairs, v, v), BF16),
        [SMEM, VMEM],
        VMEM,
        (asked, recv),
        group * CAP * cube,
        2 * cube * group * CAP,
        [pltpu.VMEM((pairs, v, v), F32)],
    )
    incoming = lax.psum_scatter(sums, "z", scatter_dimension=0, tiled=True)
    column, sums = lax.optimization_barrier((column, sums))
    reply = call(
        reply_kernel,
        jax.ShapeDtypeStruct((across, width, v, v), BF16),
        [SMEM, VMEM],
        VMEM,
        (asked, column),
        0,
        2 * cube * (pairs + group * CAP),
    )
    reply, blocks, opposite = lax.optimization_barrier((reply, blocks, opposite))
    arrived = lax.all_to_all(reply, "x", 0, 0, tiled=True)
    two = jnp.concatenate([blocks, opposite], axis=0)
    own = jnp.concatenate(
        [two, above, below, shift(two, 1), shift(two, -1)],
        axis=0,
    )
    other = lax.ppermute(own, "core", [(0, 1), (1, 0)])
    base = call(
        integral_kernel,
        jax.ShapeDtypeStruct((pairs, v, v), F32),
        [SMEM, SMEM] + [VMEM] * 5,
        VMEM,
        (domains.T, me.reshape(1), own, other, rotation, amps, energies),
        6 * pairs * blocks.shape[1] * cube,
        4 * own.size,
    )
    pulled = call(
        pull_kernel,
        jax.ShapeDtypeStruct((pairs, v, v), F32),
        [SMEM, pl.BlockSpec(memory_space=pl.ANY), VMEM],
        VMEM,
        (position, arrived.reshape(group * CAP, v, v), intersections),
        4 * entries * cube * v,
        2 * cube * (2 * entries + 2 * pairs),
        [pltpu.VMEM((entries, v, v), BF16), pltpu.SemaphoreType.DMA((entries,))],
    )
    lane = jnp.arange(ring * pairs, dtype=jnp.int32)
    spread = jnp.where(lane // pairs == me, jnp.tile(tiles, ring), 0).astype(BF16)
    note = jnp.broadcast_to(spread[None, :], (SUB, ring * pairs))
    new_amps, slabs = call(
        update_kernel,
        (
            jax.ShapeDtypeStruct((pairs, v, v), BF16),
            jax.ShapeDtypeStruct((ring, pairs + 1, SUB, v), BF16),
        ),
        [VMEM] * 7,
        (VMEM, VMEM),
        (incoming, amps, rotation, energies, base, pulled, note),
        6 * pairs * cube * v,
        2 * cube * 10 * pairs,
    )
    gathered = lax.all_to_all(slabs, AUX, 0, 0, tiled=True)
    tile_count = coeffs.shape[0] * group
    partial_sum = call(
        slab_kernel,
        jax.ShapeDtypeStruct((tile_count, SUB, v), BF16),
        [VMEM],
        VMEM,
        (gathered,),
        2 * tile_count * ring * pairs * SUB * v,
        4 * gathered.size,
        [pltpu.VMEM((ring * pairs * SUB, v), F32), pltpu.VMEM((tile_count, SUB, v), F32)],
    )
    spread_sum = lax.all_to_all(partial_sum, PAIR, 0, 0, tiled=True)
    slab = jnp.sum(spread_sum.astype(F32), axis=0).astype(BF16)
    whole = lax.all_to_all(
        jnp.broadcast_to(slab[None], (ring, SUB, v)), AUX, 0, 0, tiled=True
    ).reshape(v, v)
    factor = 1.0 / (pairs * ring)
    density = jnp.dot(whole, coeffs[0], preferred_element_type=F32) * factor
    return (new_amps, density[None])


def solution(mesh):
    fine = Mesh(mesh.devices.reshape(FINE), PAIR + AUX)

    return jax.shard_map(
        local,
        mesh=fine,
        in_specs=(
            P(PAIR + AUX, None, None),
            P(PAIR + AUX, None, None),
            P(PAIR + AUX, None, None, None),
            P(PAIR + AUX, None),
            P(PAIR + AUX, None),
            P(PAIR + AUX, None),
            P(PAIR + AUX, None),
            P(PAIR + AUX),
            P(AUX, None, None),
            P(PAIR, None, AUX),
        ),
        out_specs=(P(PAIR + AUX, None, None), P(PAIR, None, AUX)),
        check_vma=False,
    )
```

profile of v0, /device:TPU:1, one launch (start us, length us, event | category | flops | bytes accessed | tf_op | source)
XLA Modules:
  0.0 198.6 jit_solution(12930143955227724988)
XLA Ops:
  9.3 1.6 shard_map.113
  11.4 4.8 %all-to-all-start = ((s32[4,1,16]{2,1,0:T(1,128)}), s32[4,1,16]{2,1,0:T(1,128)S(1)}, u32[]{:S(2)}, u32[]{:S(2)}) async-start(s32[4,1,16]{2,1,0:T(1,128)} %bitcast.3), calls=%async_computation | async-start | bytes 4096 | tf_op jit(solution)/shard_map/all_to_all | solution.py:283
  16.3 4.5 %shard_map.114 = bf16[64,128,128]{2,1,0:T(8,128)(2,1)} custom-call(s32[32]{0:T(128)} %copy-done.12, bf16[8,128,128]{2,1,0:T(8,128)(2,1)} %amps_ref.5, bf16[8,4,128,128]{3,2,1,0:T(8,128)(2,1)} %inter_ref.3), custom_call_target="tpu_custom_call" | custom-call | flops 268435456 | bytes 3407872 | tf_op jit(solution)/shard_map/pallas_call | solution.py:29
  20.8 4.4 %all-to-all-start.1 = ((bf16[4,16,128,128]{3,2,1,0:T(8,128)(2,1)}), bf16[4,16,128,128]{3,2,1,0:T(8,128)(2,1)S(1)}, u32[]{:S(2)}, u32[]{:S(2)}) async-start(bf16[4,16,128,128]{3,2,1,0:T(8,128)(2,1)} %bitcast.24), calls=%async_computation.1 | async-start | bytes 4194304 | tf_op jit(solution)/shard_map/all_to_all | solution.py:303
  25.3 7.5 %collective-permute-start = (bf16[2,512,128]{2,1,0:T(8,128)(2,1)S(1)}, bf16[2,512,128]{2,1,0:T(8,128)(2,1)S(1)}, u32[]{:S(2)}, u32[]{:S(2)}) collective-permute-start(bf16[2,512,128]{2,1,0:T(8,128)(2,1)S(1)} %copy-done.15), channel_id=1, source_target_pairs={{0,8},{2,10},{4,12},{6,14},{8,0},{10,2},{12,4},{14,6},{1,9},{3,11}... | collective-permute-start | bytes 786440 | tf_op jit(solution)/shard_map/ppermute | solution.py:263
  32.7 7.5 %collective-permute-done = bf16[2,512,128]{2,1,0:T(8,128)(2,1)S(1)} collective-permute-done((bf16[2,512,128]{2,1,0:T(8,128)(2,1)S(1)}, bf16[2,512,128]{2,1,0:T(8,128)(2,1)S(1)}, u32[]{:S(2)}, u32[]{:S(2)}) %collective-permute-start) | collective-permute-done | bytes 262176 | tf_op jit(solution)/shard_map/ppermute | solution.py:263
  40.2 5.7 %all-to-all-done.1.recv_ref = bf16[4,16,128,128]{3,2,1,0:T(8,128)(2,1)S(1)} async-done(((bf16[4,16,128,128]{3,2,1,0:T(8,128)(2,1)}), bf16[4,16,128,128]{3,2,1,0:T(8,128)(2,1)S(1)}, u32[]{:S(2)}, u32[]{:S(2)}) %all-to-all-start.1) | async-done | bytes 2097184 | tf_op jit(solution)/shard_map/all_to_all | solution.py:303
  46.0 3.1 %shard_map.115 = bf16[64,128,128]{2,1,0:T(8,128)(2,1)} custom-call(s32[4,16]{1,0:T(4,128)S(1)} %bitcast.19, bf16[4,16,128,128]{3,2,1,0:T(8,128)(2,1)S(1)} %all-to-all-done.1.recv_ref), custom_call_target="tpu_custom_call" | custom-call | flops 1048576 | bytes 2097152 | tf_op jit(solution)/shard_map/pallas_call | solution.py:29
  49.1 6.4 %all-gather.2.cloned.1.call-done.held_ref = bf16[64,128,128]{2,1,0:T(8,128)(2,1)} async-done(((bf16[8,128,128]{2,1,0:T(8,128)(2,1)}), bf16[64,128,128]{2,1,0:T(8,128)(2,1)}) %all-gather.2.cloned.1.call-update) | async-done | bytes 2097168 | tf_op jit(solution)/shard_map/all_gather | solution.py:267
  57.1 2.1 %shard_map.116 = bf16[4,16,128,128]{3,2,1,0:T(8,128)(2,1)} custom-call(s32[4,16]{1,0:T(4,128)S(1)} %bitcast.20, bf16[64,128,128]{2,1,0:T(8,128)(2,1)S(1)} %copy-done.3), custom_call_target="tpu_custom_call" | custom-call | bytes 2359296 | tf_op jit(solution)/shard_map/pallas_call | solution.py:29
  60.7 3.1 %collective-permute-start.3 = (bf16[4,512,128]{2,1,0:T(8,128)(2,1)S(1)}, bf16[4,512,128]{2,1,0:T(8,128)(2,1)S(1)}, u32[]{:S(2)}, u32[]{:S(2)}) collective-permute-start(bf16[4,512,128]{2,1,0:T(8,128)(2,1)S(1)} %get-tuple-element.26), channel_id=1, source_target_pairs={{0,2},{2,4},{4,6},{6,8},{8,10},{10,12},{12,14},{14,0},{1,3},{3,5},... | collective-permute-start | bytes 1572872 | tf_op jit(solution)/shard_map/ppermute | solution.py:263
  63.8 4.0 %collective-permute-start.1 = (bf16[2,512,128]{2,1,0:T(8,128)(2,1)S(1)}, bf16[2,512,128]{2,1,0:T(8,128)(2,1)S(1)}, u32[]{:S(2)}, u32[]{:S(2)}) collective-permute-start(bf16[2,512,128]{2,1,0:T(8,128)(2,1)S(1)} %copy-done.15), channel_id=1, source_target_pairs={{0,4},{2,6},{4,8},{6,10},{8,12},{10,14},{12,0},{14,2},{1,5},{3,7},... | collective-permute-start | bytes 786440 | tf_op jit(solution)/shard_map/ppermute | solution.py:263
  67.8 3.4 %collective-permute-start.4 = (bf16[4,512,128]{2,1,0:T(8,128)(2,1)S(1)}, bf16[4,512,128]{2,1,0:T(8,128)(2,1)S(1)}, u32[]{:S(2)}, u32[]{:S(2)}) collective-permute-start(bf16[4,512,128]{2,1,0:T(8,128)(2,1)S(1)} %get-tuple-element.26), channel_id=1, source_target_pairs={{0,14},{2,0},{4,2},{6,4},{8,6},{10,8},{12,10},{14,12},{1,15},{3,1}... | collective-permute-start | bytes 1572872 | tf_op jit(solution)/shard_map/ppermute | solution.py:263
  71.2 2.1 %collective-permute-start.2 = (bf16[2,512,128]{2,1,0:T(8,128)(2,1)S(1)}, bf16[2,512,128]{2,1,0:T(8,128)(2,1)S(1)}, u32[]{:S(2)}, u32[]{:S(2)}) collective-permute-start(bf16[2,512,128]{2,1,0:T(8,128)(2,1)S(1)} %copy-done.15), channel_id=1, source_target_pairs={{0,12},{2,14},{4,0},{6,2},{8,4},{10,6},{12,8},{14,10},{1,13},{3,15... | collective-permute-start | bytes 786440 | tf_op jit(solution)/shard_map/ppermute | solution.py:263
  73.4 7.6 %collective-permute-done.1 = bf16[2,512,128]{2,1,0:T(8,128)(2,1)S(1)} collective-permute-done((bf16[2,512,128]{2,1,0:T(8,128)(2,1)S(1)}, bf16[2,512,128]{2,1,0:T(8,128)(2,1)S(1)}, u32[]{:S(2)}, u32[]{:S(2)}) %collective-permute-start.1) | collective-permute-done | bytes 262176 | tf_op jit(solution)/shard_map/ppermute | solution.py:263
  81.7 6.9 %collective-permute-done.2 = bf16[2,512,128]{2,1,0:T(8,128)(2,1)S(1)} collective-permute-done((bf16[2,512,128]{2,1,0:T(8,128)(2,1)S(1)}, bf16[2,512,128]{2,1,0:T(8,128)(2,1)S(1)}, u32[]{:S(2)}, u32[]{:S(2)}) %collective-permute-start.2) | collective-permute-done | bytes 262176 | tf_op jit(solution)/shard_map/ppermute | solution.py:263
  91.1 10.9 %collective-permute-start.5 = (bf16[16,512,128]{2,1,0:T(8,128)(2,1)}, bf16[16,512,128]{2,1,0:T(8,128)(2,1)}, u32[]{:S(2)}, u32[]{:S(2)}) collective-permute-start(bf16[16,512,128]{2,1,0:T(8,128)(2,1)} %constant_dynamic-update-slice_fusion.2.own_ref), channel_id=1, source_target_pairs={{0,1},{1,0},{2,3},{3,2},{4,5},{5,4},{6,7},{7,6},{8,9},{9,8},{10,11... | collective-permute-start | bytes 6291464 | tf_op jit(solution)/shard_map/ppermute | solution.py:333
  101.9 3.9 %all-to-all-start.2 = ((bf16[4,16,128,128]{3,2,1,0:T(8,128)(2,1)}), bf16[4,16,128,128]{3,2,1,0:T(8,128)(2,1)S(1)}, u32[]{:S(2)}, u32[]{:S(2)}) async-start(bf16[4,16,128,128]{3,2,1,0:T(8,128)(2,1)} %shard_map.116), calls=%async_computation.3 | async-start | bytes 4194304 | tf_op jit(solution)/shard_map/all_to_all | solution.py:327
  106.0 26.0 %all-to-all-done.2 = bf16[4,16,128,128]{3,2,1,0:T(8,128)(2,1)S(1)} async-done(((bf16[4,16,128,128]{3,2,1,0:T(8,128)(2,1)}), bf16[4,16,128,128]{3,2,1,0:T(8,128)(2,1)S(1)}, u32[]{:S(2)}, u32[]{:S(2)}) %all-to-all-start.2) | async-done | bytes 2097184 | tf_op jit(solution)/shard_map/all_to_all | solution.py:327
  132.0 3.5 %shard_map.118.pulled_ref = f32[8,128,128]{2,1,0:T(8,128)S(1)} custom-call(s32[32]{0:T(128)S(1)} %copy-done.13, bf16[64,128,128]{2,1,0:T(8,128)(2,1)S(1)} %bitcast.18, bf16[8,4,128,128]{3,2,1,0:T(8,128)(2,1)S(1)} %copy-done.1), custom_call_target="tpu_custom_call" | custom-call | flops 268435456 | bytes 2621440 | tf_op jit(solution)/shard_map/pallas_call | solution.py:29
  136.3 5.9 %shard_map.117.base_ref = f32[8,128,128]{2,1,0:T(8,128)S(1)} custom-call(s32[2,8]{1,0:T(2,128)S(1)} %bitcast.23, s32[1]{0:T(128)} %bitcast.7.me_ref, bf16[16,512,128]{2,1,0:T(8,128)(2,1)} %constant_dynamic-update-slice_fusion.2.own_ref, bf16[16,512,128]{2,1,0:T(8,128)(2,1)} %collective-permute-done.5.other_ref, bf16[8,128,128]{2,1,0:T(8,128)(2,1)S(1)} %copy-done.6, ...), custom_call_target="tpu_custom_call" | custom-call | flops 402653184 | bytes 4194304 | tf_op jit(solution)/shard_map/pallas_call | solution.py:29
  144.8 16.4 %all_to_all.37.recv_ref = bf16[16,9,8,128]{3,2,1,0:T(8,128)(2,1)S(1)} all-to-all(bf16[16,9,8,128]{3,2,1,0:T(8,128)(2,1)S(1)} %get-tuple-element.25), channel_id=1, replica_groups=mesh['x'=4,'z'=8,'y'=8,'core'=2] {'y','core'}, dimensions={0} | all-to-all | bytes 589824 | tf_op jit(solution)/shard_map/all_to_all | solution.py:368
  161.5 17.8 %all_to_all.38 = bf16[32,8,128]{2,1,0:T(8,128)(2,1)S(1)} all-to-all(bf16[32,8,128]{2,1,0:T(8,128)(2,1)S(1)} %shard_map.120), channel_id=1, replica_groups=mesh['x'=4,'z'=8,'y'=8,'core'=2] {'x','z'}, dimensions={0} | all-to-all | bytes 131072 | tf_op jit(solution)/shard_map/all_to_all | solution.py:380
  179.3 11.6 %all_to_all.39 = bf16[16,8,128]{2,1,0:T(8,128)(2,1)S(1)} all-to-all(bf16[16,8,128]{2,1,0:T(8,128)(2,1)S(1)} %broadcast_in_dim.9), channel_id=1, replica_groups=mesh['x'=4,'z'=8,'y'=8,'core'=2] {'y','core'}, dimensions={0} | all-to-all | bytes 65536 | tf_op jit(solution)/shard_map/all_to_all | solution.py:382
  (58 shorter events, 13.6 us)
Async XLA Ops:
  7.2 183.8 %copy-start = (bf16[1,128,256]{2,1,0:T(8,128)(2,1)S(1)}, bf16[1,128,256]{2,1,0:T(8,128)(2,1)}, u32[]{:S(2)}) copy-start(bf16[1,128,256]{2,1,0:T(8,128)(2,1)} %param.19) | copy-start | bytes 196612
  7.2 48.3 %all-gather.2.cloned.1.call-start = ((), (), s32[]{:S(2)}) async-start(), calls=%async_computation.8 | async-start | bytes 2359296 | tf_op jit(solution)/shard_map/all_gather | solution.py:267
  11.4 9.4 %all-to-all-start = ((s32[4,1,16]{2,1,0:T(1,128)}), s32[4,1,16]{2,1,0:T(1,128)S(1)}, u32[]{:S(2)}, u32[]{:S(2)}) async-start(s32[4,1,16]{2,1,0:T(1,128)} %bitcast.3), calls=%async_computation | async-start | bytes 4096 | tf_op jit(solution)/shard_map/all_to_all | solution.py:283
  20.8 4.4 %copy-start.15 = (bf16[2,512,128]{2,1,0:T(8,128)(2,1)S(1)}, bf16[2,512,128]{2,1,0:T(8,128)(2,1)}, u32[]{:S(2)}) copy-start(bf16[2,512,128]{2,1,0:T(8,128)(2,1)} %param.18) | copy-start | bytes 786436
  20.8 25.1 %all-to-all-start.1 = ((bf16[4,16,128,128]{3,2,1,0:T(8,128)(2,1)}), bf16[4,16,128,128]{3,2,1,0:T(8,128)(2,1)S(1)}, u32[]{:S(2)}, u32[]{:S(2)}) async-start(bf16[4,16,128,128]{3,2,1,0:T(8,128)(2,1)} %bitcast.24), calls=%async_computation.1 | async-start | bytes 4194304 | tf_op jit(solution)/shard_map/all_to_all | solution.py:303
  25.3 117.0 %reduce-scatter.2.cloned.1.call-start = ((), (), s32[]{:S(2)}) async-start(), calls=%async_computation.7 | async-start | bytes 2359296 | tf_op jit(solution)/shard_map/reduce_scatter | solution.py:315
  25.3 15.0 %collective-permute-start = (bf16[2,512,128]{2,1,0:T(8,128)(2,1)S(1)}, bf16[2,512,128]{2,1,0:T(8,128)(2,1)S(1)}, u32[]{:S(2)}, u32[]{:S(2)}) collective-permute-start(bf16[2,512,128]{2,1,0:T(8,128)(2,1)S(1)} %copy-done.15), channel_id=1, source_target_pairs={{0,8},{2,10},{4,12},{6,14},{8,0},{10,2},{12,4},{14,6},{1,9},{3,11}... | collective-permute-start | bytes 786440 | tf_op jit(solution)/shard_map/ppermute | solution.py:263
  55.5 1.6 copy-start.3
  60.7 28.6 %collective-permute-start.3 = (bf16[4,512,128]{2,1,0:T(8,128)(2,1)S(1)}, bf16[4,512,128]{2,1,0:T(8,128)(2,1)S(1)}, u32[]{:S(2)}, u32[]{:S(2)}) collective-permute-start(bf16[4,512,128]{2,1,0:T(8,128)(2,1)S(1)} %get-tuple-element.26), channel_id=1, source_target_pairs={{0,2},{2,4},{4,6},{6,8},{8,10},{10,12},{12,14},{14,0},{1,3},{3,5},... | collective-permute-start | bytes 1572872 | tf_op jit(solution)/shard_map/ppermute | solution.py:263
  63.8 17.2 %collective-permute-start.1 = (bf16[2,512,128]{2,1,0:T(8,128)(2,1)S(1)}, bf16[2,512,128]{2,1,0:T(8,128)(2,1)S(1)}, u32[]{:S(2)}, u32[]{:S(2)}) collective-permute-start(bf16[2,512,128]{2,1,0:T(8,128)(2,1)S(1)} %copy-done.15), channel_id=1, source_target_pairs={{0,4},{2,6},{4,8},{6,10},{8,12},{10,14},{12,0},{14,2},{1,5},{3,7},... | collective-permute-start | bytes 786440 | tf_op jit(solution)/shard_map/ppermute | solution.py:263
  67.8 22.3 %collective-permute-start.4 = (bf16[4,512,128]{2,1,0:T(8,128)(2,1)S(1)}, bf16[4,512,128]{2,1,0:T(8,128)(2,1)S(1)}, u32[]{:S(2)}, u32[]{:S(2)}) collective-permute-start(bf16[4,512,128]{2,1,0:T(8,128)(2,1)S(1)} %get-tuple-element.26), channel_id=1, source_target_pairs={{0,14},{2,0},{4,2},{6,4},{8,6},{10,8},{12,10},{14,12},{1,15},{3,1}... | collective-permute-start | bytes 1572872 | tf_op jit(solution)/shard_map/ppermute | solution.py:263
  71.2 17.4 %collective-permute-start.2 = (bf16[2,512,128]{2,1,0:T(8,128)(2,1)S(1)}, bf16[2,512,128]{2,1,0:T(8,128)(2,1)S(1)}, u32[]{:S(2)}, u32[]{:S(2)}) collective-permute-start(bf16[2,512,128]{2,1,0:T(8,128)(2,1)S(1)} %copy-done.15), channel_id=1, source_target_pairs={{0,12},{2,14},{4,0},{6,2},{8,4},{10,6},{12,8},{14,10},{1,13},{3,15... | collective-permute-start | bytes 786440 | tf_op jit(solution)/shard_map/ppermute | solution.py:263
  91.1 14.8 %copy-start.16 = (s32[8]{0:T(128)S(1)}, s32[8]{0:T(128)}, u32[]{:S(2)}) copy-start(s32[8]{0:T(128)} %param.17) | copy-start | bytes 100
  91.1 40.9 %copy-start.1 = (bf16[8,4,128,128]{3,2,1,0:T(8,128)(2,1)S(1)}, bf16[8,4,128,128]{3,2,1,0:T(8,128)(2,1)}, u32[]{:S(2)}) copy-start(bf16[8,4,128,128]{3,2,1,0:T(8,128)(2,1)} %inter_ref.3) | copy-start | bytes 3145732
  91.1 40.9 %copy-start.13 = (s32[32]{0:T(128)S(1)}, s32[32]{0:T(128)}, u32[]{:S(2)}) copy-start(s32[32]{0:T(128)} %copy-done.12) | copy-start | bytes 388
  91.1 45.2 %collective-permute-start.5 = (bf16[16,512,128]{2,1,0:T(8,128)(2,1)}, bf16[16,512,128]{2,1,0:T(8,128)(2,1)}, u32[]{:S(2)}, u32[]{:S(2)}) collective-permute-start(bf16[16,512,128]{2,1,0:T(8,128)(2,1)} %constant_dynamic-update-slice_fusion.2.own_ref), channel_id=1, source_target_pairs={{0,1},{1,0},{2,3},{3,2},{4,5},{5,4},{6,7},{7,6},{8,9},{9,8},{10,11... | collective-permute-start | bytes 6291464 | tf_op jit(solution)/shard_map/ppermute | solution.py:333
  101.9 30.0 %all-to-all-start.2 = ((bf16[4,16,128,128]{3,2,1,0:T(8,128)(2,1)}), bf16[4,16,128,128]{3,2,1,0:T(8,128)(2,1)S(1)}, u32[]{:S(2)}, u32[]{:S(2)}) async-start(bf16[4,16,128,128]{3,2,1,0:T(8,128)(2,1)} %shard_map.116), calls=%async_computation.3 | async-start | bytes 4194304 | tf_op jit(solution)/shard_map/all_to_all | solution.py:327
  105.8 30.4 %copy-start.2 = (bf16[8,128,128]{2,1,0:T(8,128)(2,1)S(1)}, bf16[8,128,128]{2,1,0:T(8,128)(2,1)}, u32[]{:S(2)}) copy-start(bf16[8,128,128]{2,1,0:T(8,128)(2,1)} %amps_ref.5) | copy-start | bytes 786436
  105.8 30.4 %copy-start.9 = (f32[8,128]{1,0:T(8,128)S(1)}, f32[8,128]{1,0:T(8,128)}, u32[]{:S(2)}) copy-start(f32[8,128]{1,0:T(8,128)} %energy_ref.3) | copy-start | bytes 12292
  105.8 30.4 %copy-start.14 = (s32[8,2]{0,1:T(2,128)S(1)}, s32[8,2]{0,1:T(2,128)}, u32[]{:S(2)}) copy-start(s32[8,2]{0,1:T(2,128)} %param.14) | copy-start | bytes 196
  132.0 4.3 %copy-start.6 = (bf16[8,128,128]{2,1,0:T(8,128)(2,1)S(1)}, bf16[8,128,128]{2,1,0:T(8,128)(2,1)}, u32[]{:S(2)}) copy-start(bf16[8,128,128]{2,1,0:T(8,128)(2,1)} %rot_ref.3) | copy-start | bytes 786436
  136.3 6.0 %copy-start.5 = (f32[8,128,128]{2,1,0:T(8,128)S(1)}, f32[8,128,128]{2,1,0:T(8,128)}, u32[]{:S(2)}) copy-start(f32[8,128,128]{2,1,0:T(8,128)} %copy-done.4) | copy-start | bytes 1572868
  136.3 6.0 %copy-start.7 = (bf16[8,128,128]{2,1,0:T(8,128)(2,1)S(1)}, bf16[8,128,128]{2,1,0:T(8,128)(2,1)}, u32[]{:S(2)}) copy-start(bf16[8,128,128]{2,1,0:T(8,128)(2,1)} %rot_ref.3) | copy-start | bytes 786436
  142.3 1.0 copy-start.8
  (4 other events, 2.7 us)
Sparse Core Ops, SparseCore 0:
  10.1 45.3 all-gather.1
  58.3 44.1 reduce-scatter.1
where the time goes:
time: 199 us
  waiting for transfers between devices  60.8 us (31%)
  blocking collectives  45.8 us (23%)
  starting transfers between devices  44.2 us (22%)
  Pallas kernels  22.6 us (11%)
  between operations  14.3 us (7%)
  local copies, waits for them, and re-layouts  10.1 us (5%)
    all_to_all x1, waiting for transfers between devices, local(): arrived = lax.all_to_all(reply, 'x', 0, 0, tiled=True)  26 us
    pallas_call x8, Pallas kernels, call(): pl.pallas_call(kernel, out_shape=out_shape, in_specs=in_specs, out_specs=...  22.6 us
    ppermute x5, waiting for transfers between devices, shift(): lax.ppermute(value, 'y', [(j, (j + k) % chips) for j in range(chips)])  22 us
    ppermute x5, starting transfers between devices, shift(): lax.ppermute(value, 'y', [(j, (j + k) % chips) for j in range(chips)])  20.1 us
    all_to_all x1, blocking collectives, local(): spread_sum = lax.all_to_all(partial_sum, PAIR, 0, 0, tiled=True)  17.8 us
    all_to_all x1, blocking collectives, local(): gathered = lax.all_to_all(slabs, AUX, 0, 0, tiled=True)  16.4 us
    all_to_all x1, blocking collectives, local(): lax.all_to_all(jnp.broadcast_to(slab[None], (ring, SUB, v)), AUX, 0, 0, t...  11.6 us
    ppermute x1, starting transfers between devices, local(): other = lax.ppermute(own, 'core', [(0, 1), (1, 0)])  10.9 us
  transfers between devices with their start and end apart: 11, of which 6 were waited for; matrix products, arithmetic and copies ran while one was open for 2% of the time, Pallas kernels for 10%

commit v1 on v0

--- a/solution.py
+++ b/solution.py
@@ -39,16 +39,43 @@
     )(*args)
 
 
-def plan_kernel(owner_ref, slot_ref, want_ref, pos_ref, count):
-    neighbours, pairs = owner_ref.shape
-    rows, width = want_ref.shape
-
-    @pl.loop(0, rows)
+def push_kernel(owner_ref, slot_ref, amps_ref, inter_ref, send_ref, pos_ref, *scratch):
+    amps_buf, inter_buf, block_buf, note_buf, count, sems, amps_sems, inter_sems, note_sem = scratch
+    pairs, neighbours, v, _ = inter_ref.shape
+    rows = send_ref.shape[0]
+    width = send_ref.shape[1] // v
+    step = 2
+
+    def get(p):
+        return (
+            pltpu.make_async_copy(amps_ref.at[p], amps_buf.at[p], amps_sems.at[p]),
+            pltpu.make_async_copy(inter_ref.at[p], inter_buf.at[p], inter_sems.at[p]),
+        )
+
+    for p in range(pairs):
+        for copy in get(p):
+            copy.start()
+
+    def put(e):
+        at = pos_ref[e]
+        place = pl.ds(pl.multiple_of(lax.rem(at, width) * v, v), v)
+        return pltpu.make_async_copy(
+            block_buf.at[e], send_ref.at[at // width, place, :], sems.at[e]
+        )
+
+    def put_notes():
+        return pltpu.make_async_copy(note_buf, send_ref.at[:, pl.ds(width * v, SUB), :], note_sem)
+
+    def put_all(g):
+        for i in range(step * neighbours):
+            put(g * step * neighbours + i).start()
+
+    note_buf[...] = jnp.zeros(note_buf.shape, BF16)
+    lane = lax.broadcasted_iota(jnp.int32, (SUB, v), 1)
+
+    @pl.loop(0, rows * width // CAP)
     def _(o):
-        for i in range(width):
-            want_ref[o, i] = 0
-        for i in range(width // CAP):
-            count[o * (width // CAP) + i] = 0
+        count[o] = 0
 
     @pl.loop(0, pairs)
     def _(p):
@@ -58,30 +85,9 @@
             count[o] = r + 1
             at = o * CAP + r
             pos_ref[p * neighbours + n] = at
-            want_ref[at // width, lax.rem(at, width)] = slot_ref[n, p] + 1
-
-
-def push_kernel(pos_ref, amps_ref, inter_ref, send_ref, *scratch):
-    amps_buf, inter_buf, block_buf, sems, amps_sems, inter_sems = scratch
-    pairs, neighbours, v, _ = inter_ref.shape
-    step = 2
-
-    def get(p):
-        return (
-            pltpu.make_async_copy(amps_ref.at[p], amps_buf.at[p], amps_sems.at[p]),
-            pltpu.make_async_copy(inter_ref.at[p], inter_buf.at[p], inter_sems.at[p]),
-        )
-
-    def put(e):
-        return pltpu.make_async_copy(block_buf.at[e], send_ref.at[pos_ref[e]], sems.at[e])
-
-    def put_all(g):
-        for i in range(step * neighbours):
-            put(g * step * neighbours + i).start()
-
-    for p in range(pairs):
-        for copy in get(p):
-            copy.start()
+            d = at // width
+            mark = jnp.where(lane == lax.rem(at, width), slot_ref[n, p] + 1, 0)
+            note_buf[d] = note_buf[d] + mark.astype(F32).astype(BF16)
 
     @pl.loop(0, pairs // step)
     def _(g):
@@ -102,26 +108,41 @@
         def _():
             put_all(g - 1)
 
+    put_notes().start()
     put_all(pairs // step - 1)
+    put_notes().wait()
 
     @pl.loop(0, pairs * neighbours)
     def _(e):
         put(e).wait()
 
 
-def reply_kernel(want_ref, held_ref, out_ref):
+def reply_kernel(
+    want_ref, me_ref, first_ref, own_ref, far_ref, up_ref, down_ref, up2_ref, down2_ref, out_ref, held
+):
     rows, width = want_ref.shape
-    per = held_ref.shape[0] // (width // CAP)
+    depth = width // CAP
+    low = first_ref.shape[0] // depth
+    high = own_ref.shape[0]
+    per = low + high
+    pieces = [own_ref, far_ref, up_ref, down_ref, up2_ref, up2_ref, down2_ref, down2_ref]
+    offsets = [0, 0, 0, 0, 0, high, 0, high]
+    for z in range(depth):
+        held[z * per : z * per + low] = first_ref[z * low : (z + 1) * low]
+    for k in range(depth):
+        z = lax.rem(me_ref[0] - k + depth, depth)
+        p = PLACE[k]
+        held[pl.ds(z * per + low, high)] = pieces[p][offsets[p] : offsets[p] + high]
 
     @pl.loop(0, rows)
     def _(d):
         for i in range(width):
-            out_ref[d, i] = held_ref[i // CAP * per + jnp.maximum(want_ref[d, i] - 1, 0)]
+            out_ref[d, i] = held[i // CAP * per + jnp.maximum(want_ref[d, i] - 1, 0)]
 
 
 def sum_kernel(want_ref, recv_ref, out_ref, total):
     rows, width = want_ref.shape
-    per = total.shape[0]
+    per, v, _ = total.shape
 
     @pl.loop(0, width // CAP)
     def _(o):
@@ -129,10 +150,11 @@
         for d in range(rows):
             for r in range(CAP):
                 s = want_ref[d, o * CAP + r]
+                place = pl.ds(pl.multiple_of((o * CAP + r) * v, v), v)
 
                 @pl.when(s > 0)
                 def _():
-                    total[s - 1] += recv_ref[d, o * CAP + r].astype(F32)
+                    total[s - 1] += recv_ref[d, place, :].astype(F32)
 
         out_ref[pl.ds(o * per, per)] = total[...].astype(BF16)
 
@@ -259,49 +281,51 @@
 
     assert chips == len(PLACE)
 
-    def shift(value, k):
-        return lax.ppermute(value, "y", [(j, (j + k) % chips) for j in range(chips)])
-
-    opposite = shift(blocks, 4)
-    above, below = shift(blocks, 2), shift(blocks, -2)
-    column = lax.all_gather(amps, "z", axis=0, tiled=True)
+    depth = lax.axis_size("z")
+    assert depth == len(PLACE)
+
+    def shift(value, axis, k):
+        size = lax.axis_size(axis)
+        return lax.ppermute(value, axis, [(j, (j + k) % size) for j in range(size)])
+
+    opposite = shift(blocks, "y", 4)
+    above, below = shift(blocks, "y", 2), shift(blocks, "y", -2)
+    low = pairs // 2
+    column = lax.all_gather(amps[:low], "z", axis=0, tiled=True)
+    high = amps[low:]
+    zfar = shift(high, "z", 4)
+    zup2, zdown2 = shift(high, "z", 2), shift(high, "z", -2)
+    both = jnp.concatenate([high, zfar], axis=0)
+    zup1, zdown1 = shift(both, "z", 1), shift(both, "z", -1)
     across = lax.axis_size("x")
     width = CAP * group // across
-    want, position = call(
-        plan_kernel,
+    send, position = call(
+        push_kernel,
         (
-            jax.ShapeDtypeStruct((across, width), jnp.int32),
+            jax.ShapeDtypeStruct((across, width * v + SUB, v), BF16),
             jax.ShapeDtypeStruct((entries,), jnp.int32),
         ),
-        [SMEM, SMEM],
-        (SMEM, SMEM),
-        (owners.T, slots.T),
-        0,
-        1024,
-        [pltpu.SMEM((group,), jnp.int32)],
-    )
-    asked = lax.all_to_all(want, "x", 0, 0, tiled=True)
-    send = call(
-        push_kernel,
-        jax.ShapeDtypeStruct((group * CAP, v, v), BF16),
-        [SMEM, HBM, HBM],
-        HBM,
-        (position, amps, intersections),
+        [SMEM, SMEM, HBM, HBM],
+        (HBM, SMEM),
+        (owners.T, slots.T, amps, intersections),
         4 * entries * cube * v,
         2 * cube * (pairs + entries + group * CAP),
         [
             pltpu.VMEM((pairs, v, v), BF16),
             pltpu.VMEM((pairs, neighbours, v, v), BF16),
             pltpu.VMEM((entries, v, v), BF16),
+            pltpu.VMEM((across, SUB, v), BF16),
+            pltpu.SMEM((group,), jnp.int32),
             pltpu.SemaphoreType.DMA((entries,)),
             pltpu.SemaphoreType.DMA((pairs,)),
             pltpu.SemaphoreType.DMA((pairs,)),
+            pltpu.SemaphoreType.DMA,
         ],
         58,
     )
-    send, asked = lax.optimization_barrier((send, asked))
-    recv = lax.all_to_all(send.reshape(across, width, v, v), "x", 0, 0, tiled=True)
+    recv = lax.all_to_all(send, "x", 0, 0, tiled=True)
     recv, opposite = lax.optimization_barrier((recv, opposite))
+    asked = recv[:, width * v, :width].astype(jnp.int32)
     sums = call(
         sum_kernel,
         jax.ShapeDtypeStruct((group // across * pairs, v, v), BF16),
@@ -311,23 +335,28 @@
         group * CAP * cube,
         2 * cube * group * CAP,
         [pltpu.VMEM((pairs, v, v), F32)],
+        48,
     )
     incoming = lax.psum_scatter(sums, "z", scatter_dimension=0, tiled=True)
-    column, sums = lax.optimization_barrier((column, sums))
+    asked, sums = lax.optimization_barrier((asked, sums))
     reply = call(
         reply_kernel,
         jax.ShapeDtypeStruct((across, width, v, v), BF16),
-        [SMEM, VMEM],
+        [SMEM, SMEM] + [VMEM] * 7,
         VMEM,
-        (asked, column),
+        (
+            asked, lax.axis_index("z").astype(jnp.int32).reshape(1),
+            column, high, zfar, zup2, zdown2, zup1, zdown1,
+        ),
         0,
-        2 * cube * (pairs + group * CAP),
+        4 * cube * group * CAP,
+        [pltpu.VMEM((depth * pairs, v, v), BF16)],
     )
     reply, blocks, opposite = lax.optimization_barrier((reply, blocks, opposite))
     arrived = lax.all_to_all(reply, "x", 0, 0, tiled=True)
     two = jnp.concatenate([blocks, opposite], axis=0)
     own = jnp.concatenate(
-        [two, above, below, shift(two, 1), shift(two, -1)],
+        [two, above, below, shift(two, "y", 1), shift(two, "y", -1)],
         axis=0,
     )
     other = lax.ppermute(own, "core", [(0, 1), (1, 0)])

time: 199 us -> 229 us (1.15)
  starting transfers between devices: 44.2 us -> 73.6 us
  waiting for transfers between devices: 60.8 us -> 67.6 us
  blocking collectives: 45.8 us -> 40.1 us
    ppermute x5 -> x10, starting transfers between devices: 20.1 us -> 53.8 us  [shift(): return lax.ppermute(value, axis, [(j, (j + k) % size) for j in range(size)])]
    ppermute x5 -> x10, waiting for transfers between devices: 22 us -> 36.1 us  [shift(): return lax.ppermute(value, axis, [(j, (j + k) % size) for j in range(size)])]
    all_gather x1, waiting for transfers between devices: 6.36 us -> 0.01 us  [local(): column = lax.all_gather(amps[:low], 'z', axis=0, tiled=True)]
    all_to_all x1, blocking collectives: 17.8 us -> 12.3 us  [local(): spread_sum = lax.all_to_all(partial_sum, PAIR, 0, 0, tiled=True)]
    all_to_all x2 -> x1, starting transfers between devices: 9.24 us -> 4.99 us  [local(): recv = lax.all_to_all(send, 'x', 0, 0, tiled=True)]
    pallas_call x8 -> x7, Pallas kernels: 22.6 us -> 20.5 us  [call(): pl.pallas_call(kernel, out_shape=out_shape, in_specs=in_specs, out_specs=...]
    unnamed x38 -> x34, local copies, waits for them, and re-layouts: 8.31 us -> 7.44 us
    all_to_all x2 -> x1, waiting for transfers between devices: 5.71 us -> 5.21 us  [local(): recv = lax.all_to_all(send, 'x', 0, 0, tiled=True)]
  transfers between devices with their start and end apart: 11 -> 15, of which waited for: 6 -> 8; matrix products, arithmetic and copies ran while one was open for 2% -> 2% of each run, Pallas kernels for 10% -> 8%
where the time goes in v1:
time: 229 us; the launch traced here: 228 us
  starting transfers between devices  73.6 us (32%)
  waiting for transfers between devices  67.6 us (30%)
  blocking collectives  40.1 us (18%)
  Pallas kernels  20.5 us (9%)
  between operations  14.4 us (6%)
  local copies, waits for them, and re-layouts  10.8 us (5%)
    ppermute x10, starting transfers between devices, shift(): return lax.ppermute(value, axis, [(j, (j + k) % size) for j in range(size)])  53.8 us
    ppermute x10, waiting for transfers between devices, shift(): return lax.ppermute(value, axis, [(j, (j + k) % size) for j in range(size)])  36.1 us
    all_to_all x1, waiting for transfers between devices, local(): arrived = lax.all_to_all(reply, 'x', 0, 0, tiled=True)  26.2 us
    pallas_call x7, Pallas kernels, call(): pl.pallas_call(kernel, out_shape=out_shape, in_specs=in_specs, out_specs=...  20.5 us
    all_to_all x1, blocking collectives, local(): gathered = lax.all_to_all(slabs, AUX, 0, 0, tiled=True)  16.2 us
    all_to_all x1, blocking collectives, local(): spread_sum = lax.all_to_all(partial_sum, PAIR, 0, 0, tiled=True)  12.3 us
    all_to_all x1, blocking collectives, local(): lax.all_to_all(jnp.broadcast_to(slab[None], (ring, SUB, v)), AUX, 0, 0, t...  11.6 us
    ppermute x1, starting transfers between devices, local(): other = lax.ppermute(own, 'core', [(0, 1), (1, 0)])  11.1 us
  transfers between devices with their start and end apart: 15, of which 8 were waited for; matrix products, arithmetic and copies ran while one was open for 2% of the time, Pallas kernels for 8%

profile of v1, /device:TPU:1, one launch (start us, length us, event | category | flops | bytes accessed | tf_op | source)
XLA Modules:
  0.0 227.9 jit_solution(487366349893106580)
XLA Ops:
  8.9 5.3 %shard_map.113 = (bf16[4,2056,128]{2,1,0:T(8,128)(2,1)}, s32[32]{0:T(128)}) custom-call(s32[4,8]{1,0:T(4,128)} %bitcast.19, s32[4,8]{1,0:T(4,128)} %bitcast.20, bf16[8,128,128]{2,1,0:T(8,128)(2,1)} %amps_ref.5, bf16[8,4,128,128]{3,2,1,0:T(8,128)(2,1)} %inter_ref.3), custom_call_target="tpu_custom_call" | custom-call | flops 268435456 | bytes 3407872 | tf_op jit(solution)/shard_map/pallas_call | solution.py:29
  14.2 5.0 %all-to-all-start = ((bf16[4,2056,128]{2,1,0:T(8,128)(2,1)}), bf16[4,2056,128]{2,1,0:T(8,128)(2,1)S(1)}, u32[]{:S(2)}, u32[]{:S(2)}) async-start(bf16[4,2056,128]{2,1,0:T(8,128)(2,1)} %get-tuple-element.12), calls=%async_computation | async-start | bytes 4210688 | tf_op jit(solution)/shard_map/all_to_all | solution.py:326
  19.2 7.5 %collective-permute-start = (bf16[2,512,128]{2,1,0:T(8,128)(2,1)S(1)}, bf16[2,512,128]{2,1,0:T(8,128)(2,1)S(1)}, u32[]{:S(2)}, u32[]{:S(2)}) collective-permute-start(bf16[2,512,128]{2,1,0:T(8,128)(2,1)S(1)} %copy-done.13), channel_id=1, source_target_pairs={{0,8},{2,10},{4,12},{6,14},{8,0},{10,2},{12,4},{14,6},{1,9},{3,11}... | collective-permute-start | bytes 786440 | tf_op jit(solution)/shard_map/ppermute | solution.py:289
  26.7 8.0 %collective-permute-done = bf16[2,512,128]{2,1,0:T(8,128)(2,1)S(1)} collective-permute-done((bf16[2,512,128]{2,1,0:T(8,128)(2,1)S(1)}, bf16[2,512,128]{2,1,0:T(8,128)(2,1)S(1)}, u32[]{:S(2)}, u32[]{:S(2)}) %collective-permute-start) | collective-permute-done | bytes 262176 | tf_op jit(solution)/shard_map/ppermute | solution.py:289
  34.7 5.2 %all-to-all-done.recv_ref = bf16[4,2056,128]{2,1,0:T(8,128)(2,1)S(1)} async-done(((bf16[4,2056,128]{2,1,0:T(8,128)(2,1)}), bf16[4,2056,128]{2,1,0:T(8,128)(2,1)S(1)}, u32[]{:S(2)}, u32[]{:S(2)}) %all-to-all-start) | async-done | bytes 2105376 | tf_op jit(solution)/shard_map/all_to_all | solution.py:326
  43.0 15.6 %collective-permute-start.1 = (bf16[4,128,128]{2,1,0:T(8,128)(2,1)S(1)}, bf16[4,128,128]{2,1,0:T(8,128)(2,1)S(1)}, u32[]{:S(2)}, u32[]{:S(2)}) collective-permute-start(bf16[4,128,128]{2,1,0:T(8,128)(2,1)S(1)} %get-tuple-element.26.own_ref), channel_id=1, source_target_pairs={{0,64},{16,80},{32,96},{48,112},{64,0},{80,16},{96,32},{112,48},{1... | collective-permute-start | bytes 393224 | tf_op jit(solution)/shard_map/ppermute | solution.py:289
  58.6 2.4 %collective-permute-done.1.far_ref = bf16[4,128,128]{2,1,0:T(8,128)(2,1)S(1)} collective-permute-done((bf16[4,128,128]{2,1,0:T(8,128)(2,1)S(1)}, bf16[4,128,128]{2,1,0:T(8,128)(2,1)S(1)}, u32[]{:S(2)}, u32[]{:S(2)}) %collective-permute-start.1) | collective-permute-done | bytes 131104 | tf_op jit(solution)/shard_map/ppermute | solution.py:289
  61.1 7.9 %collective-permute-start.5 = (bf16[8,128,128]{2,1,0:T(8,128)(2,1)S(1)}, bf16[8,128,128]{2,1,0:T(8,128)(2,1)S(1)}, u32[]{:S(2)}, u32[]{:S(2)}) collective-permute-start(bf16[8,128,128]{2,1,0:T(8,128)(2,1)S(1)} %pad_maximum_fusion), channel_id=1, source_target_pairs={{0,112},{16,0},{32,16},{48,32},{64,48},{80,64},{96,80},{112,96},{1... | collective-permute-start | bytes 786440 | tf_op jit(solution)/shard_map/ppermute | solution.py:289
  70.9 5.8 %collective-permute-start.3 = (bf16[4,128,128]{2,1,0:T(8,128)(2,1)S(1)}, bf16[4,128,128]{2,1,0:T(8,128)(2,1)S(1)}, u32[]{:S(2)}, u32[]{:S(2)}) collective-permute-start(bf16[4,128,128]{2,1,0:T(8,128)(2,1)S(1)} %get-tuple-element.26.own_ref), channel_id=1, source_target_pairs={{0,96},{16,112},{32,0},{48,16},{64,32},{80,48},{96,64},{112,80},{1... | collective-permute-start | bytes 393224 | tf_op jit(solution)/shard_map/ppermute | solution.py:289
  78.6 5.3 %collective-permute-done.3.down_ref = bf16[4,128,128]{2,1,0:T(8,128)(2,1)S(1)} collective-permute-done((bf16[4,128,128]{2,1,0:T(8,128)(2,1)S(1)}, bf16[4,128,128]{2,1,0:T(8,128)(2,1)S(1)}, u32[]{:S(2)}, u32[]{:S(2)}) %collective-permute-start.3) | collective-permute-done | bytes 131104 | tf_op jit(solution)/shard_map/ppermute | solution.py:289
  83.9 6.2 %collective-permute-done.2.up_ref = bf16[4,128,128]{2,1,0:T(8,128)(2,1)S(1)} collective-permute-done((bf16[4,128,128]{2,1,0:T(8,128)(2,1)S(1)}, bf16[4,128,128]{2,1,0:T(8,128)(2,1)S(1)}, u32[]{:S(2)}, u32[]{:S(2)}) %collective-permute-start.2) | collective-permute-done | bytes 131104 | tf_op jit(solution)/shard_map/ppermute | solution.py:289
  95.2 3.3 %collective-permute-start.8 = (bf16[4,512,128]{2,1,0:T(8,128)(2,1)S(1)}, bf16[4,512,128]{2,1,0:T(8,128)(2,1)S(1)}, u32[]{:S(2)}, u32[]{:S(2)}) collective-permute-start(bf16[4,512,128]{2,1,0:T(8,128)(2,1)S(1)} %get-tuple-element.22), channel_id=1, source_target_pairs={{0,2},{2,4},{4,6},{6,8},{8,10},{10,12},{12,14},{14,0},{1,3},{3,5},... | collective-permute-start | bytes 1572872 | tf_op jit(solution)/shard_map/ppermute | solution.py:289
  98.4 4.2 %collective-permute-start.6 = (bf16[2,512,128]{2,1,0:T(8,128)(2,1)S(1)}, bf16[2,512,128]{2,1,0:T(8,128)(2,1)S(1)}, u32[]{:S(2)}, u32[]{:S(2)}) collective-permute-start(bf16[2,512,128]{2,1,0:T(8,128)(2,1)S(1)} %copy-done.13), channel_id=1, source_target_pairs={{0,4},{2,6},{4,8},{6,10},{8,12},{10,14},{12,0},{14,2},{1,5},{3,7},... | collective-permute-start | bytes 786440 | tf_op jit(solution)/shard_map/ppermute | solution.py:289
  102.7 3.3 %collective-permute-start.9 = (bf16[4,512,128]{2,1,0:T(8,128)(2,1)S(1)}, bf16[4,512,128]{2,1,0:T(8,128)(2,1)S(1)}, u32[]{:S(2)}, u32[]{:S(2)}) collective-permute-start(bf16[4,512,128]{2,1,0:T(8,128)(2,1)S(1)} %get-tuple-element.22), channel_id=1, source_target_pairs={{0,14},{2,0},{4,2},{6,4},{8,6},{10,8},{12,10},{14,12},{1,15},{3,1}... | collective-permute-start | bytes 1572872 | tf_op jit(solution)/shard_map/ppermute | solution.py:289
  108.4 7.1 %collective-permute-done.6 = bf16[2,512,128]{2,1,0:T(8,128)(2,1)S(1)} collective-permute-done((bf16[2,512,128]{2,1,0:T(8,128)(2,1)S(1)}, bf16[2,512,128]{2,1,0:T(8,128)(2,1)S(1)}, u32[]{:S(2)}, u32[]{:S(2)}) %collective-permute-start.6) | collective-permute-done | bytes 262176 | tf_op jit(solution)/shard_map/ppermute | solution.py:289
  116.2 7.1 %collective-permute-done.7 = bf16[2,512,128]{2,1,0:T(8,128)(2,1)S(1)} collective-permute-done((bf16[2,512,128]{2,1,0:T(8,128)(2,1)S(1)}, bf16[2,512,128]{2,1,0:T(8,128)(2,1)S(1)}, u32[]{:S(2)}, u32[]{:S(2)}) %collective-permute-start.7) | collective-permute-done | bytes 262176 | tf_op jit(solution)/shard_map/ppermute | solution.py:289
  125.7 11.1 %collective-permute-start.10 = (bf16[16,512,128]{2,1,0:T(8,128)(2,1)}, bf16[16,512,128]{2,1,0:T(8,128)(2,1)}, u32[]{:S(2)}, u32[]{:S(2)}) collective-permute-start(bf16[16,512,128]{2,1,0:T(8,128)(2,1)} %constant_dynamic-update-slice_fusion.2.own_ref), channel_id=1, source_target_pairs={{0,1},{1,0},{2,3},{3,2},{4,5},{5,4},{6,7},{7,6},{8,9},{9,8},{10,11... | collective-permute-start | bytes 6291464 | tf_op jit(solution)/shard_map/ppermute | solution.py:362
  136.9 3.6 %all-to-all-start.1 = ((bf16[4,16,128,128]{3,2,1,0:T(8,128)(2,1)}), bf16[4,16,128,128]{3,2,1,0:T(8,128)(2,1)S(1)}, u32[]{:S(2)}, u32[]{:S(2)}) async-start(bf16[4,16,128,128]{3,2,1,0:T(8,128)(2,1)} %shard_map.115), calls=%async_computation.2 | async-start | bytes 4194304 | tf_op jit(solution)/shard_map/all_to_all | solution.py:356
  140.7 26.2 %all-to-all-done.1 = bf16[4,16,128,128]{3,2,1,0:T(8,128)(2,1)S(1)} async-done(((bf16[4,16,128,128]{3,2,1,0:T(8,128)(2,1)}), bf16[4,16,128,128]{3,2,1,0:T(8,128)(2,1)S(1)}, u32[]{:S(2)}, u32[]{:S(2)}) %all-to-all-start.1) | async-done | bytes 2097184 | tf_op jit(solution)/shard_map/all_to_all | solution.py:356
  166.9 3.5 %shard_map.117.pulled_ref = f32[8,128,128]{2,1,0:T(8,128)S(1)} custom-call(s32[32]{0:T(128)S(1)} %copy-done.12, bf16[64,128,128]{2,1,0:T(8,128)(2,1)S(1)} %bitcast.15, bf16[8,4,128,128]{3,2,1,0:T(8,128)(2,1)S(1)} %copy-done.2), custom_call_target="tpu_custom_call" | custom-call | flops 268435456 | bytes 2621440 | tf_op jit(solution)/shard_map/pallas_call | solution.py:29
  171.3 5.9 %shard_map.116.base_ref = f32[8,128,128]{2,1,0:T(8,128)S(1)} custom-call(s32[2,8]{1,0:T(2,128)S(1)} %bitcast.18, s32[1]{0:T(128)} %bitcast.4.me_ref, bf16[16,512,128]{2,1,0:T(8,128)(2,1)} %constant_dynamic-update-slice_fusion.2.own_ref, bf16[16,512,128]{2,1,0:T(8,128)(2,1)} %collective-permute-done.10.other_ref, bf16[8,128,128]{2,1,0:T(8,128)(2,1)S(1)} %copy-done.7, ...), custom_call_target="tpu_custom_call" | custom-call | flops 402653184 | bytes 4194304 | tf_op jit(solution)/shard_map/pallas_call | solution.py:29
  179.8 16.2 %all_to_all.25.recv_ref = bf16[16,9,8,128]{3,2,1,0:T(8,128)(2,1)S(1)} all-to-all(bf16[16,9,8,128]{3,2,1,0:T(8,128)(2,1)S(1)} %get-tuple-element.21), channel_id=1, replica_groups=mesh['x'=4,'z'=8,'y'=8,'core'=2] {'y','core'}, dimensions={0} | all-to-all | bytes 589824 | tf_op jit(solution)/shard_map/all_to_all | solution.py:397
  196.2 12.3 %all_to_all.26 = bf16[32,8,128]{2,1,0:T(8,128)(2,1)S(1)} all-to-all(bf16[32,8,128]{2,1,0:T(8,128)(2,1)S(1)} %shard_map.119), channel_id=1, replica_groups=mesh['x'=4,'z'=8,'y'=8,'core'=2] {'x','z'}, dimensions={0} | all-to-all | bytes 131072 | tf_op jit(solution)/shard_map/all_to_all | solution.py:409
  208.6 11.6 %all_to_all.27 = bf16[16,8,128]{2,1,0:T(8,128)(2,1)S(1)} all-to-all(bf16[16,8,128]{2,1,0:T(8,128)(2,1)S(1)} %broadcast_in_dim.9), channel_id=1, replica_groups=mesh['x'=4,'z'=8,'y'=8,'core'=2] {'y','core'}, dimensions={0} | all-to-all | bytes 65536 | tf_op jit(solution)/shard_map/all_to_all | solution.py:411
  (64 shorter events, 23.8 us)
Async XLA Ops:
  7.2 213.1 %copy-start = (bf16[1,128,256]{2,1,0:T(8,128)(2,1)S(1)}, bf16[1,128,256]{2,1,0:T(8,128)(2,1)}, u32[]{:S(2)}) copy-start(bf16[1,128,256]{2,1,0:T(8,128)(2,1)} %param.19) | copy-start | bytes 196612
  7.2 83.0 %all-gather.2.cloned.1.call-start = ((), (), s32[]{:S(2)}) async-start(), calls=%async_computation.7 | async-start | bytes 1179648 | tf_op jit(solution)/shard_map/all_gather | solution.py:294
  14.2 25.6 %all-to-all-start = ((bf16[4,2056,128]{2,1,0:T(8,128)(2,1)}), bf16[4,2056,128]{2,1,0:T(8,128)(2,1)S(1)}, u32[]{:S(2)}, u32[]{:S(2)}) async-start(bf16[4,2056,128]{2,1,0:T(8,128)(2,1)} %get-tuple-element.12), calls=%async_computation | async-start | bytes 4210688 | tf_op jit(solution)/shard_map/all_to_all | solution.py:326
  19.2 158.0 %reduce-scatter.2.cloned.1.call-start = ((), (), s32[]{:S(2)}) async-start(), calls=%async_computation.6 | async-start | bytes 2359296 | tf_op jit(solution)/shard_map/reduce_scatter | solution.py:340
  19.2 15.4 %collective-permute-start = (bf16[2,512,128]{2,1,0:T(8,128)(2,1)S(1)}, bf16[2,512,128]{2,1,0:T(8,128)(2,1)S(1)}, u32[]{:S(2)}, u32[]{:S(2)}) collective-permute-start(bf16[2,512,128]{2,1,0:T(8,128)(2,1)S(1)} %copy-done.13), channel_id=1, source_target_pairs={{0,8},{2,10},{4,12},{6,14},{8,0},{10,2},{12,4},{14,6},{1,9},{3,11}... | collective-permute-start | bytes 786440 | tf_op jit(solution)/shard_map/ppermute | solution.py:289
  43.0 18.0 %collective-permute-start.1 = (bf16[4,128,128]{2,1,0:T(8,128)(2,1)S(1)}, bf16[4,128,128]{2,1,0:T(8,128)(2,1)S(1)}, u32[]{:S(2)}, u32[]{:S(2)}) collective-permute-start(bf16[4,128,128]{2,1,0:T(8,128)(2,1)S(1)} %get-tuple-element.26.own_ref), channel_id=1, source_target_pairs={{0,64},{16,80},{32,96},{48,112},{64,0},{80,16},{96,32},{112,48},{1... | collective-permute-start | bytes 393224 | tf_op jit(solution)/shard_map/ppermute | solution.py:289
  61.1 29.1 %collective-permute-start.5 = (bf16[8,128,128]{2,1,0:T(8,128)(2,1)S(1)}, bf16[8,128,128]{2,1,0:T(8,128)(2,1)S(1)}, u32[]{:S(2)}, u32[]{:S(2)}) collective-permute-start(bf16[8,128,128]{2,1,0:T(8,128)(2,1)S(1)} %pad_maximum_fusion), channel_id=1, source_target_pairs={{0,112},{16,0},{32,16},{48,32},{64,48},{80,64},{96,80},{112,96},{1... | collective-permute-start | bytes 786440 | tf_op jit(solution)/shard_map/ppermute | solution.py:289
  69.0 21.1 %collective-permute-start.4 = (bf16[8,128,128]{2,1,0:T(8,128)(2,1)S(1)}, bf16[8,128,128]{2,1,0:T(8,128)(2,1)S(1)}, u32[]{:S(2)}, u32[]{:S(2)}) collective-permute-start(bf16[8,128,128]{2,1,0:T(8,128)(2,1)S(1)} %pad_maximum_fusion), channel_id=1, source_target_pairs={{0,16},{16,32},{32,48},{48,64},{64,80},{80,96},{96,112},{112,0},{1... | collective-permute-start | bytes 786440 | tf_op jit(solution)/shard_map/ppermute | solution.py:289
  70.9 13.0 %collective-permute-start.3 = (bf16[4,128,128]{2,1,0:T(8,128)(2,1)S(1)}, bf16[4,128,128]{2,1,0:T(8,128)(2,1)S(1)}, u32[]{:S(2)}, u32[]{:S(2)}) collective-permute-start(bf16[4,128,128]{2,1,0:T(8,128)(2,1)S(1)} %get-tuple-element.26.own_ref), channel_id=1, source_target_pairs={{0,96},{16,112},{32,0},{48,16},{64,32},{80,48},{96,64},{112,80},{1... | collective-permute-start | bytes 393224 | tf_op jit(solution)/shard_map/ppermute | solution.py:289
  76.7 13.4 %collective-permute-start.2 = (bf16[4,128,128]{2,1,0:T(8,128)(2,1)S(1)}, bf16[4,128,128]{2,1,0:T(8,128)(2,1)S(1)}, u32[]{:S(2)}, u32[]{:S(2)}) collective-permute-start(bf16[4,128,128]{2,1,0:T(8,128)(2,1)S(1)} %get-tuple-element.26.own_ref), channel_id=1, source_target_pairs={{0,32},{16,48},{32,64},{48,80},{64,96},{80,112},{96,0},{112,16},{1... | collective-permute-start | bytes 393224 | tf_op jit(solution)/shard_map/ppermute | solution.py:289
  95.2 28.8 %collective-permute-start.8 = (bf16[4,512,128]{2,1,0:T(8,128)(2,1)S(1)}, bf16[4,512,128]{2,1,0:T(8,128)(2,1)S(1)}, u32[]{:S(2)}, u32[]{:S(2)}) collective-permute-start(bf16[4,512,128]{2,1,0:T(8,128)(2,1)S(1)} %get-tuple-element.22), channel_id=1, source_target_pairs={{0,2},{2,4},{4,6},{6,8},{8,10},{10,12},{12,14},{14,0},{1,3},{3,5},... | collective-permute-start | bytes 1572872 | tf_op jit(solution)/shard_map/ppermute | solution.py:289
  98.4 17.1 %collective-permute-start.6 = (bf16[2,512,128]{2,1,0:T(8,128)(2,1)S(1)}, bf16[2,512,128]{2,1,0:T(8,128)(2,1)S(1)}, u32[]{:S(2)}, u32[]{:S(2)}) collective-permute-start(bf16[2,512,128]{2,1,0:T(8,128)(2,1)S(1)} %copy-done.13), channel_id=1, source_target_pairs={{0,4},{2,6},{4,8},{6,10},{8,12},{10,14},{12,0},{14,2},{1,5},{3,7},... | collective-permute-start | bytes 786440 | tf_op jit(solution)/shard_map/ppermute | solution.py:289
  102.7 22.2 %collective-permute-start.9 = (bf16[4,512,128]{2,1,0:T(8,128)(2,1)S(1)}, bf16[4,512,128]{2,1,0:T(8,128)(2,1)S(1)}, u32[]{:S(2)}, u32[]{:S(2)}) collective-permute-start(bf16[4,512,128]{2,1,0:T(8,128)(2,1)S(1)} %get-tuple-element.22), channel_id=1, source_target_pairs={{0,14},{2,0},{4,2},{6,4},{8,6},{10,8},{12,10},{14,12},{1,15},{3,1}... | collective-permute-start | bytes 1572872 | tf_op jit(solution)/shard_map/ppermute | solution.py:289
  106.0 17.2 %collective-permute-start.7 = (bf16[2,512,128]{2,1,0:T(8,128)(2,1)S(1)}, bf16[2,512,128]{2,1,0:T(8,128)(2,1)S(1)}, u32[]{:S(2)}, u32[]{:S(2)}) collective-permute-start(bf16[2,512,128]{2,1,0:T(8,128)(2,1)S(1)} %copy-done.13), channel_id=1, source_target_pairs={{0,12},{2,14},{4,0},{6,2},{8,4},{10,6},{12,8},{14,10},{1,13},{3,15... | collective-permute-start | bytes 786440 | tf_op jit(solution)/shard_map/ppermute | solution.py:289
  125.7 14.8 %copy-start.14 = (s32[8]{0:T(128)S(1)}, s32[8]{0:T(128)}, u32[]{:S(2)}) copy-start(s32[8]{0:T(128)} %param.17) | copy-start | bytes 100
  125.7 41.2 %copy-start.2 = (bf16[8,4,128,128]{3,2,1,0:T(8,128)(2,1)S(1)}, bf16[8,4,128,128]{3,2,1,0:T(8,128)(2,1)}, u32[]{:S(2)}) copy-start(bf16[8,4,128,128]{3,2,1,0:T(8,128)(2,1)} %inter_ref.3) | copy-start | bytes 3145732
  125.7 41.2 %copy-start.12 = (s32[32]{0:T(128)S(1)}, s32[32]{0:T(128)}, u32[]{:S(2)}) copy-start(s32[32]{0:T(128)} %get-tuple-element.18.pos_ref) | copy-start | bytes 388
  125.7 45.5 %collective-permute-start.10 = (bf16[16,512,128]{2,1,0:T(8,128)(2,1)}, bf16[16,512,128]{2,1,0:T(8,128)(2,1)}, u32[]{:S(2)}, u32[]{:S(2)}) collective-permute-start(bf16[16,512,128]{2,1,0:T(8,128)(2,1)} %constant_dynamic-update-slice_fusion.2.own_ref), channel_id=1, source_target_pairs={{0,1},{1,0},{2,3},{3,2},{4,5},{5,4},{6,7},{7,6},{8,9},{9,8},{10,11... | collective-permute-start | bytes 6291464 | tf_op jit(solution)/shard_map/ppermute | solution.py:362
  136.9 30.0 %all-to-all-start.1 = ((bf16[4,16,128,128]{3,2,1,0:T(8,128)(2,1)}), bf16[4,16,128,128]{3,2,1,0:T(8,128)(2,1)S(1)}, u32[]{:S(2)}, u32[]{:S(2)}) async-start(bf16[4,16,128,128]{3,2,1,0:T(8,128)(2,1)} %shard_map.115), calls=%async_computation.2 | async-start | bytes 4194304 | tf_op jit(solution)/shard_map/all_to_all | solution.py:356
  140.5 30.7 %copy-start.3 = (bf16[8,128,128]{2,1,0:T(8,128)(2,1)S(1)}, bf16[8,128,128]{2,1,0:T(8,128)(2,1)}, u32[]{:S(2)}) copy-start(bf16[8,128,128]{2,1,0:T(8,128)(2,1)} %amps_ref.5) | copy-start | bytes 786436
  140.5 30.7 %copy-start.10 = (f32[8,128]{1,0:T(8,128)S(1)}, f32[8,128]{1,0:T(8,128)}, u32[]{:S(2)}) copy-start(f32[8,128]{1,0:T(8,128)} %energy_ref.3) | copy-start | bytes 12292
  140.6 30.7 %copy-start.11 = (s32[8,2]{0,1:T(2,128)S(1)}, s32[8,2]{0,1:T(2,128)}, u32[]{:S(2)}) copy-start(s32[8,2]{0,1:T(2,128)} %param.14) | copy-start | bytes 196
  171.2 6.0 %copy-start.5 = (f32[8,128,128]{2,1,0:T(8,128)S(1)}, f32[8,128,128]{2,1,0:T(8,128)}, u32[]{:S(2)}) copy-start(f32[8,128,128]{2,1,0:T(8,128)} %copy-done.4) | copy-start | bytes 1572868
  171.2 6.0 %copy-start.8 = (bf16[8,128,128]{2,1,0:T(8,128)(2,1)S(1)}, bf16[8,128,128]{2,1,0:T(8,128)(2,1)}, u32[]{:S(2)}) copy-start(bf16[8,128,128]{2,1,0:T(8,128)(2,1)} %rot_ref.3) | copy-start | bytes 786436
  (6 other events, 13.7 us)
Sparse Core Ops, SparseCore 0:
  10.6 42.8 all-gather.1
  56.4 51.9 reduce-scatter.1

commit v2 on v1

--- a/solution.py
+++ b/solution.py
@@ -117,27 +117,14 @@
         put(e).wait()
 
 
-def reply_kernel(
-    want_ref, me_ref, first_ref, own_ref, far_ref, up_ref, down_ref, up2_ref, down2_ref, out_ref, held
-):
+def reply_kernel(want_ref, held_ref, out_ref):
     rows, width = want_ref.shape
-    depth = width // CAP
-    low = first_ref.shape[0] // depth
-    high = own_ref.shape[0]
-    per = low + high
-    pieces = [own_ref, far_ref, up_ref, down_ref, up2_ref, up2_ref, down2_ref, down2_ref]
-    offsets = [0, 0, 0, 0, 0, high, 0, high]
-    for z in range(depth):
-        held[z * per : z * per + low] = first_ref[z * low : (z + 1) * low]
-    for k in range(depth):
-        z = lax.rem(me_ref[0] - k + depth, depth)
-        p = PLACE[k]
-        held[pl.ds(z * per + low, high)] = pieces[p][offsets[p] : offsets[p] + high]
+    per = held_ref.shape[0] // (width // CAP)
 
     @pl.loop(0, rows)
     def _(d):
         for i in range(width):
-            out_ref[d, i] = held[i // CAP * per + jnp.maximum(want_ref[d, i] - 1, 0)]
+            out_ref[d, i] = held_ref[i // CAP * per + jnp.maximum(want_ref[d, i] - 1, 0)]
 
 
 def sum_kernel(want_ref, recv_ref, out_ref, total):
@@ -157,6 +144,14 @@
                     total[s - 1] += recv_ref[d, place, :].astype(F32)
 
         out_ref[pl.ds(o * per, per)] = total[...].astype(BF16)
+
+
+def pack_kernel(*refs):
+    out_ref = refs[-1]
+    at = 0
+    for ref in refs[:-1]:
+        out_ref[at : at + ref.shape[0]] = ref[...]
+        at += ref.shape[0]
 
 
 def denominator(energy_ref, p):
@@ -281,22 +276,15 @@
 
     assert chips == len(PLACE)
 
-    depth = lax.axis_size("z")
-    assert depth == len(PLACE)
-
     def shift(value, axis, k):
         size = lax.axis_size(axis)
         return lax.ppermute(value, axis, [(j, (j + k) % size) for j in range(size)])
 
     opposite = shift(blocks, "y", 4)
     above, below = shift(blocks, "y", 2), shift(blocks, "y", -2)
-    low = pairs // 2
-    column = lax.all_gather(amps[:low], "z", axis=0, tiled=True)
-    high = amps[low:]
-    zfar = shift(high, "z", 4)
-    zup2, zdown2 = shift(high, "z", 2), shift(high, "z", -2)
-    both = jnp.concatenate([high, zfar], axis=0)
-    zup1, zdown1 = shift(both, "z", 1), shift(both, "z", -1)
+    two = jnp.concatenate([blocks, opposite], axis=0)
+    left, right = shift(two, "y", 1), shift(two, "y", -1)
+    column = lax.all_gather(amps, "z", axis=0, tiled=True)
     across = lax.axis_size("x")
     width = CAP * group // across
     send, position = call(
@@ -324,7 +312,6 @@
         58,
     )
     recv = lax.all_to_all(send, "x", 0, 0, tiled=True)
-    recv, opposite = lax.optimization_barrier((recv, opposite))
     asked = recv[:, width * v, :width].astype(jnp.int32)
     sums = call(
         sum_kernel,
@@ -338,26 +325,25 @@
         48,
     )
     incoming = lax.psum_scatter(sums, "z", scatter_dimension=0, tiled=True)
-    asked, sums = lax.optimization_barrier((asked, sums))
+    column, sums = lax.optimization_barrier((column, sums))
     reply = call(
         reply_kernel,
         jax.ShapeDtypeStruct((across, width, v, v), BF16),
-        [SMEM, SMEM] + [VMEM] * 7,
-        VMEM,
-        (
-            asked, lax.axis_index("z").astype(jnp.int32).reshape(1),
-            column, high, zfar, zup2, zdown2, zup1, zdown1,
-        ),
+        [SMEM, VMEM],
+        VMEM,
+        (asked, column),
         0,
         4 * cube * group * CAP,
-        [pltpu.VMEM((depth * pairs, v, v), BF16)],
-    )
-    reply, blocks, opposite = lax.optimization_barrier((reply, blocks, opposite))
+    )
     arrived = lax.all_to_all(reply, "x", 0, 0, tiled=True)
-    two = jnp.concatenate([blocks, opposite], axis=0)
-    own = jnp.concatenate(
-        [two, above, below, shift(two, "y", 1), shift(two, "y", -1)],
-        axis=0,
+    own = call(
+        pack_kernel,
+        jax.ShapeDtypeStruct((ring * blocks.shape[0] // CORES,) + blocks.shape[1:], BF16),
+        [VMEM] * 5,
+        VMEM,
+        (two, above, below, left, right),
+        0,
+        4 * two.size * chips // 2,
     )
     other = lax.ppermute(own, "core", [(0, 1), (1, 0)])
     base = call(

time: 229 us -> 203 us (0.89)
  blocking collectives: 40.1 us -> 73.5 us
  starting transfers between devices: 73.6 us -> 40.2 us
  waiting for transfers between devices: 67.6 us -> 40.7 us
    all_to_all x0 -> x1, blocking collectives: none -> 25.6 us  [local(): recv = lax.all_to_all(send, 'x', 0, 0, tiled=True)]
    ppermute x10 -> x5, starting transfers between devices: 53.8 us -> 32.8 us  [shift(): return lax.ppermute(value, axis, [(j, (j + k) % size) for j in range(size)])]
    ppermute x10 -> x5, waiting for transfers between devices: 36.1 us -> 21.5 us  [shift(): return lax.ppermute(value, axis, [(j, (j + k) % size) for j in range(size)])]
    all_to_all x1, waiting for transfers between devices: 26.2 us -> 18.5 us  [local(): arrived = lax.all_to_all(reply, 'x', 0, 0, tiled=True)]
    ppermute x1, starting transfers between devices: 11.1 us -> 3.61 us  [local(): other = lax.ppermute(own, 'core', [(0, 1), (1, 0)])]
    all_to_all x1, blocking collectives: 12.3 us -> 19.8 us  [local(): spread_sum = lax.all_to_all(partial_sum, PAIR, 0, 0, tiled=True)]
    all_to_all x1 -> x0, waiting for transfers between devices: 5.21 us -> none  [local(): recv = lax.all_to_all(send, 'x', 0, 0, tiled=True)]
    all_to_all x1 -> x0, starting transfers between devices: 4.99 us -> none  [local(): recv = lax.all_to_all(send, 'x', 0, 0, tiled=True)]
  transfers between devices with their start and end apart: 15 -> 9, of which waited for: 8 -> 4; matrix products, arithmetic and copies ran while one was open for 2% -> 0% of each run, Pallas kernels for 8% -> 10%
where the time goes in v2:
time: 203 us; the launch traced here: 202 us
  blocking collectives  73.5 us (36%)
  waiting for transfers between devices  40.7 us (20%)
  starting transfers between devices  40.2 us (20%)
  Pallas kernels  21.8 us (11%)
  between operations  14.3 us (7%)
  local copies, waits for them, and re-layouts  10.5 us (5%)
    ppermute x5, starting transfers between devices, shift(): return lax.ppermute(value, axis, [(j, (j + k) % size) for j in range(size)])  32.8 us
    all_to_all x1, blocking collectives, local(): recv = lax.all_to_all(send, 'x', 0, 0, tiled=True)  25.6 us
    pallas_call x8, Pallas kernels, call(): pl.pallas_call(kernel, out_shape=out_shape, in_specs=in_specs, out_specs=...  21.8 us
    ppermute x5, waiting for transfers between devices, shift(): return lax.ppermute(value, axis, [(j, (j + k) % size) for j in range(size)])  21.5 us
    all_to_all x1, blocking collectives, local(): spread_sum = lax.all_to_all(partial_sum, PAIR, 0, 0, tiled=True)  19.8 us
    all_to_all x1, waiting for transfers between devices, local(): arrived = lax.all_to_all(reply, 'x', 0, 0, tiled=True)  18.5 us
    all_to_all x1, blocking collectives, local(): gathered = lax.all_to_all(slabs, AUX, 0, 0, tiled=True)  16.6 us
    all_to_all x1, blocking collectives, local(): lax.all_to_all(jnp.broadcast_to(slab[None], (ring, SUB, v)), AUX, 0, 0, t...  11.6 us
  transfers between devices with their start and end apart: 9, of which 4 were waited for; matrix products, arithmetic and copies ran while one was open for 0% of the time, Pallas kernels for 10%

profile of v2, /device:TPU:1, one launch (start us, length us, event | category | flops | bytes accessed | tf_op | source)
XLA Modules:
  0.0 202.0 jit_solution(11091652067727862010)
XLA Ops:
  8.0 5.3 %shard_map.113 = (bf16[4,2056,128]{2,1,0:T(8,128)(2,1)}, s32[32]{0:T(128)}) custom-call(s32[4,8]{1,0:T(4,128)} %bitcast.18, s32[4,8]{1,0:T(4,128)} %bitcast.19, bf16[8,128,128]{2,1,0:T(8,128)(2,1)} %amps_ref.5, bf16[8,4,128,128]{3,2,1,0:T(8,128)(2,1)} %inter_ref.3), custom_call_target="tpu_custom_call" | custom-call | flops 268435456 | bytes 3407872 | tf_op jit(solution)/shard_map/pallas_call | solution.py:29
  13.3 25.6 %all_to_all.25.recv_ref = bf16[4,2056,128]{2,1,0:T(8,128)(2,1)S(1)} all-to-all(bf16[4,2056,128]{2,1,0:T(8,128)(2,1)} %get-tuple-element.7), channel_id=1, replica_groups=mesh['x'=4,'z'=8,'y'=8,'core'=2] {'x'}, dimensions={0} | all-to-all | bytes 4210688 | tf_op jit(solution)/shard_map/all_to_all | solution.py:314
  38.9 3.1 %shard_map.114 = bf16[64,128,128]{2,1,0:T(8,128)(2,1)} custom-call(s32[4,16]{1,0:T(4,128)S(1)} %bitcast.15, bf16[4,2056,128]{2,1,0:T(8,128)(2,1)S(1)} %all_to_all.25.recv_ref), custom_call_target="tpu_custom_call" | custom-call | flops 1048576 | bytes 2097152 | tf_op jit(solution)/shard_map/pallas_call | solution.py:29
  42.9 12.2 %collective-permute-start = (bf16[2,512,128]{2,1,0:T(8,128)(2,1)S(1)}, bf16[2,512,128]{2,1,0:T(8,128)(2,1)S(1)}, u32[]{:S(2)}, u32[]{:S(2)}) collective-permute-start(bf16[2,512,128]{2,1,0:T(8,128)(2,1)S(1)} %copy-done.15), channel_id=1, source_target_pairs={{0,8},{2,10},{4,12},{6,14},{8,0},{10,2},{12,4},{14,6},{1,9},{3,11}... | collective-permute-start | bytes 786440 | tf_op jit(solution)/shard_map/ppermute | solution.py:281
  55.2 4.7 %collective-permute-done = bf16[2,512,128]{2,1,0:T(8,128)(2,1)S(1)} collective-permute-done((bf16[2,512,128]{2,1,0:T(8,128)(2,1)S(1)}, bf16[2,512,128]{2,1,0:T(8,128)(2,1)S(1)}, u32[]{:S(2)}, u32[]{:S(2)}) %collective-permute-start) | collective-permute-done | bytes 262176 | tf_op jit(solution)/shard_map/ppermute | solution.py:281
  59.9 5.7 %collective-permute-start.3 = (bf16[4,512,128]{2,1,0:T(8,128)(2,1)S(1)}, bf16[4,512,128]{2,1,0:T(8,128)(2,1)S(1)}, u32[]{:S(2)}, u32[]{:S(2)}) collective-permute-start(bf16[4,512,128]{2,1,0:T(8,128)(2,1)S(1)} %constant_dynamic-update-slice_fusion.refs_0_), channel_id=1, source_target_pairs={{0,2},{2,4},{4,6},{6,8},{8,10},{10,12},{12,14},{14,0},{1,3},{3,5},... | collective-permute-start | bytes 1572872 | tf_op jit(solution)/shard_map/ppermute | solution.py:281
  65.6 7.4 %collective-permute-start.4 = (bf16[4,512,128]{2,1,0:T(8,128)(2,1)S(1)}, bf16[4,512,128]{2,1,0:T(8,128)(2,1)S(1)}, u32[]{:S(2)}, u32[]{:S(2)}) collective-permute-start(bf16[4,512,128]{2,1,0:T(8,128)(2,1)S(1)} %constant_dynamic-update-slice_fusion.refs_0_), channel_id=1, source_target_pairs={{0,14},{2,0},{4,2},{6,4},{8,6},{10,8},{12,10},{14,12},{1,15},{3,1}... | collective-permute-start | bytes 1572872 | tf_op jit(solution)/shard_map/ppermute | solution.py:281
  73.1 3.8 %collective-permute-start.1 = (bf16[2,512,128]{2,1,0:T(8,128)(2,1)S(1)}, bf16[2,512,128]{2,1,0:T(8,128)(2,1)S(1)}, u32[]{:S(2)}, u32[]{:S(2)}) collective-permute-start(bf16[2,512,128]{2,1,0:T(8,128)(2,1)S(1)} %copy-done.15), channel_id=1, source_target_pairs={{0,4},{2,6},{4,8},{6,10},{8,12},{10,14},{12,0},{14,2},{1,5},{3,7},... | collective-permute-start | bytes 786440 | tf_op jit(solution)/shard_map/ppermute | solution.py:281
  76.8 3.6 %collective-permute-start.2 = (bf16[2,512,128]{2,1,0:T(8,128)(2,1)S(1)}, bf16[2,512,128]{2,1,0:T(8,128)(2,1)S(1)}, u32[]{:S(2)}, u32[]{:S(2)}) collective-permute-start(bf16[2,512,128]{2,1,0:T(8,128)(2,1)S(1)} %copy-done.15), channel_id=1, source_target_pairs={{0,12},{2,14},{4,0},{6,2},{8,4},{10,6},{12,8},{14,10},{1,13},{3,15... | collective-permute-start | bytes 786440 | tf_op jit(solution)/shard_map/ppermute | solution.py:281
  80.5 9.3 %collective-permute-done.1.refs_1_ = bf16[2,512,128]{2,1,0:T(8,128)(2,1)S(1)} collective-permute-done((bf16[2,512,128]{2,1,0:T(8,128)(2,1)S(1)}, bf16[2,512,128]{2,1,0:T(8,128)(2,1)S(1)}, u32[]{:S(2)}, u32[]{:S(2)}) %collective-permute-start.1) | collective-permute-done | bytes 262176 | tf_op jit(solution)/shard_map/ppermute | solution.py:281
  89.7 7.6 %collective-permute-done.2.refs_2_ = bf16[2,512,128]{2,1,0:T(8,128)(2,1)S(1)} collective-permute-done((bf16[2,512,128]{2,1,0:T(8,128)(2,1)S(1)}, bf16[2,512,128]{2,1,0:T(8,128)(2,1)S(1)}, u32[]{:S(2)}, u32[]{:S(2)}) %collective-permute-start.2) | collective-permute-done | bytes 262176 | tf_op jit(solution)/shard_map/ppermute | solution.py:281
  97.3 1.5 shard_map.115.own_ref
  98.8 3.6 %collective-permute-start.5 = (bf16[16,512,128]{2,1,0:T(8,128)(2,1)}, bf16[16,512,128]{2,1,0:T(8,128)(2,1)}, u32[]{:S(2)}, u32[]{:S(2)}) collective-permute-start(bf16[16,512,128]{2,1,0:T(8,128)(2,1)} %shard_map.115.own_ref), channel_id=1, source_target_pairs={{0,1},{1,0},{2,3},{3,2},{4,5},{5,4},{6,7},{7,6},{8,9},{9,8},{10,11... | collective-permute-start | bytes 6291464 | tf_op jit(solution)/shard_map/ppermute | solution.py:348
  102.4 1.6 copy-done.4
  104.8 1.3 copy-done.1
  106.1 3.8 %all-to-all-start.1 = ((bf16[4,16,128,128]{3,2,1,0:T(8,128)(2,1)}), bf16[4,16,128,128]{3,2,1,0:T(8,128)(2,1)S(1)}, u32[]{:S(2)}, u32[]{:S(2)}) async-start(bf16[4,16,128,128]{3,2,1,0:T(8,128)(2,1)} %copy-done.1), calls=%async_computation.2 | async-start | bytes 4194304 | tf_op jit(solution)/shard_map/all_to_all | solution.py:338
  111.0 5.9 %shard_map.116.base_ref = f32[8,128,128]{2,1,0:T(8,128)S(1)} custom-call(s32[2,8]{1,0:T(2,128)S(1)} %bitcast.17, s32[1]{0:T(128)} %bitcast.4.me_ref, bf16[16,512,128]{2,1,0:T(8,128)(2,1)} %shard_map.115.own_ref, bf16[16,512,128]{2,1,0:T(8,128)(2,1)} %collective-permute-done.5.other_ref, bf16[8,128,128]{2,1,0:T(8,128)(2,1)S(1)} %copy-done.9, ...), custom_call_target="tpu_custom_call" | custom-call | flops 402653184 | bytes 4194304 | tf_op jit(solution)/shard_map/pallas_call | solution.py:29
  117.7 18.5 %all-to-all-done.1 = bf16[4,16,128,128]{3,2,1,0:T(8,128)(2,1)S(1)} async-done(((bf16[4,16,128,128]{3,2,1,0:T(8,128)(2,1)}), bf16[4,16,128,128]{3,2,1,0:T(8,128)(2,1)S(1)}, u32[]{:S(2)}, u32[]{:S(2)}) %all-to-all-start.1) | async-done | bytes 2097184 | tf_op jit(solution)/shard_map/all_to_all | solution.py:338
  136.2 3.5 %shard_map.118.pulled_ref = f32[8,128,128]{2,1,0:T(8,128)S(1)} custom-call(s32[32]{0:T(128)S(1)} %copy-done.14, bf16[64,128,128]{2,1,0:T(8,128)(2,1)S(1)} %bitcast.14, bf16[8,4,128,128]{3,2,1,0:T(8,128)(2,1)S(1)} %copy-done.2), custom_call_target="tpu_custom_call" | custom-call | flops 268435456 | bytes 2621440 | tf_op jit(solution)/shard_map/pallas_call | solution.py:29
  140.5 1.0 copy-done.6
  144.5 1.6 shard_map.119
  146.0 16.6 %all_to_all.26.recv_ref = bf16[16,9,8,128]{3,2,1,0:T(8,128)(2,1)S(1)} all-to-all(bf16[16,9,8,128]{3,2,1,0:T(8,128)(2,1)S(1)} %get-tuple-element.11), channel_id=1, replica_groups=mesh['x'=4,'z'=8,'y'=8,'core'=2] {'y','core'}, dimensions={0} | all-to-all | bytes 589824 | tf_op jit(solution)/shard_map/all_to_all | solution.py:383
  162.9 19.8 %all_to_all.27 = bf16[32,8,128]{2,1,0:T(8,128)(2,1)S(1)} all-to-all(bf16[32,8,128]{2,1,0:T(8,128)(2,1)S(1)} %shard_map.120), channel_id=1, replica_groups=mesh['x'=4,'z'=8,'y'=8,'core'=2] {'x','z'}, dimensions={0} | all-to-all | bytes 131072 | tf_op jit(solution)/shard_map/all_to_all | solution.py:395
  182.7 11.6 %all_to_all.28 = bf16[16,8,128]{2,1,0:T(8,128)(2,1)S(1)} all-to-all(bf16[16,8,128]{2,1,0:T(8,128)(2,1)S(1)} %broadcast_in_dim.9), channel_id=1, replica_groups=mesh['x'=4,'z'=8,'y'=8,'core'=2] {'y','core'}, dimensions={0} | all-to-all | bytes 65536 | tf_op jit(solution)/shard_map/all_to_all | solution.py:397
  (52 shorter events, 9.2 us)
Async XLA Ops:
  7.2 187.2 %copy-start = (bf16[1,128,256]{2,1,0:T(8,128)(2,1)S(1)}, bf16[1,128,256]{2,1,0:T(8,128)(2,1)}, u32[]{:S(2)}) copy-start(bf16[1,128,256]{2,1,0:T(8,128)(2,1)} %param.19) | copy-start | bytes 196612
  7.2 95.3 %all-gather.2.cloned.1.call-start = ((), (), s32[]{:S(2)}) async-start(), calls=%async_computation.7 | async-start | bytes 2359296 | tf_op jit(solution)/shard_map/all_gather | solution.py:287
  7.9 132.6 %reduce-scatter.2.cloned.1.call-start = ((), (), s32[]{:S(2)}) async-start(), calls=%async_computation.6 | async-start | bytes 2359296 | tf_op jit(solution)/shard_map/reduce_scatter | solution.py:327
  42.0 0.9 copy-start.15
  42.9 16.9 %collective-permute-start = (bf16[2,512,128]{2,1,0:T(8,128)(2,1)S(1)}, bf16[2,512,128]{2,1,0:T(8,128)(2,1)S(1)}, u32[]{:S(2)}, u32[]{:S(2)}) collective-permute-start(bf16[2,512,128]{2,1,0:T(8,128)(2,1)S(1)} %copy-done.15), channel_id=1, source_target_pairs={{0,8},{2,10},{4,12},{6,14},{8,0},{10,2},{12,4},{14,6},{1,9},{3,11}... | collective-permute-start | bytes 786440 | tf_op jit(solution)/shard_map/ppermute | solution.py:281
  59.9 37.4 %collective-permute-start.3 = (bf16[4,512,128]{2,1,0:T(8,128)(2,1)S(1)}, bf16[4,512,128]{2,1,0:T(8,128)(2,1)S(1)}, u32[]{:S(2)}, u32[]{:S(2)}) collective-permute-start(bf16[4,512,128]{2,1,0:T(8,128)(2,1)S(1)} %constant_dynamic-update-slice_fusion.refs_0_), channel_id=1, source_target_pairs={{0,2},{2,4},{4,6},{6,8},{8,10},{10,12},{12,14},{14,0},{1,3},{3,5},... | collective-permute-start | bytes 1572872 | tf_op jit(solution)/shard_map/ppermute | solution.py:281
  65.6 31.7 %collective-permute-start.4 = (bf16[4,512,128]{2,1,0:T(8,128)(2,1)S(1)}, bf16[4,512,128]{2,1,0:T(8,128)(2,1)S(1)}, u32[]{:S(2)}, u32[]{:S(2)}) collective-permute-start(bf16[4,512,128]{2,1,0:T(8,128)(2,1)S(1)} %constant_dynamic-update-slice_fusion.refs_0_), channel_id=1, source_target_pairs={{0,14},{2,0},{4,2},{6,4},{8,6},{10,8},{12,10},{14,12},{1,15},{3,1}... | collective-permute-start | bytes 1572872 | tf_op jit(solution)/shard_map/ppermute | solution.py:281
  73.1 16.7 %collective-permute-start.1 = (bf16[2,512,128]{2,1,0:T(8,128)(2,1)S(1)}, bf16[2,512,128]{2,1,0:T(8,128)(2,1)S(1)}, u32[]{:S(2)}, u32[]{:S(2)}) collective-permute-start(bf16[2,512,128]{2,1,0:T(8,128)(2,1)S(1)} %copy-done.15), channel_id=1, source_target_pairs={{0,4},{2,6},{4,8},{6,10},{8,12},{10,14},{12,0},{14,2},{1,5},{3,7},... | collective-permute-start | bytes 786440 | tf_op jit(solution)/shard_map/ppermute | solution.py:281
  76.8 20.5 %collective-permute-start.2 = (bf16[2,512,128]{2,1,0:T(8,128)(2,1)S(1)}, bf16[2,512,128]{2,1,0:T(8,128)(2,1)S(1)}, u32[]{:S(2)}, u32[]{:S(2)}) collective-permute-start(bf16[2,512,128]{2,1,0:T(8,128)(2,1)S(1)} %copy-done.15), channel_id=1, source_target_pairs={{0,12},{2,14},{4,0},{6,2},{8,4},{10,6},{12,8},{14,10},{1,13},{3,15... | collective-permute-start | bytes 786440 | tf_op jit(solution)/shard_map/ppermute | solution.py:281
  98.8 11.2 %collective-permute-start.5 = (bf16[16,512,128]{2,1,0:T(8,128)(2,1)}, bf16[16,512,128]{2,1,0:T(8,128)(2,1)}, u32[]{:S(2)}, u32[]{:S(2)}) collective-permute-start(bf16[16,512,128]{2,1,0:T(8,128)(2,1)} %shard_map.115.own_ref), channel_id=1, source_target_pairs={{0,1},{1,0},{2,3},{3,2},{4,5},{5,4},{6,7},{7,6},{8,9},{9,8},{10,11... | collective-permute-start | bytes 6291464 | tf_op jit(solution)/shard_map/ppermute | solution.py:348
  102.4 1.6 copy-start.4
  104.8 1.3 copy-start.1
  106.1 3.8 %copy-start.16 = (s32[8]{0:T(128)S(1)}, s32[8]{0:T(128)}, u32[]{:S(2)}) copy-start(s32[8]{0:T(128)} %param.17) | copy-start | bytes 100
  106.1 3.9 %copy-start.3 = (bf16[8,128,128]{2,1,0:T(8,128)(2,1)S(1)}, bf16[8,128,128]{2,1,0:T(8,128)(2,1)}, u32[]{:S(2)}) copy-start(bf16[8,128,128]{2,1,0:T(8,128)(2,1)} %amps_ref.5) | copy-start | bytes 786436
  106.1 3.9 %copy-start.12 = (f32[8,128]{1,0:T(8,128)S(1)}, f32[8,128]{1,0:T(8,128)}, u32[]{:S(2)}) copy-start(f32[8,128]{1,0:T(8,128)} %energy_ref.3) | copy-start | bytes 12292
  106.1 3.9 %copy-start.13 = (s32[8,2]{0,1:T(2,128)S(1)}, s32[8,2]{0,1:T(2,128)}, u32[]{:S(2)}) copy-start(s32[8,2]{0,1:T(2,128)} %param.14) | copy-start | bytes 196
  106.1 30.1 %all-to-all-start.1 = ((bf16[4,16,128,128]{3,2,1,0:T(8,128)(2,1)}), bf16[4,16,128,128]{3,2,1,0:T(8,128)(2,1)S(1)}, u32[]{:S(2)}, u32[]{:S(2)}) async-start(bf16[4,16,128,128]{3,2,1,0:T(8,128)(2,1)} %copy-done.1), calls=%async_computation.2 | async-start | bytes 4194304 | tf_op jit(solution)/shard_map/all_to_all | solution.py:338
  110.0 1.0 copy-start.9
  111.0 25.2 %copy-start.2 = (bf16[8,4,128,128]{3,2,1,0:T(8,128)(2,1)S(1)}, bf16[8,4,128,128]{3,2,1,0:T(8,128)(2,1)}, u32[]{:S(2)}) copy-start(bf16[8,4,128,128]{3,2,1,0:T(8,128)(2,1)} %inter_ref.3) | copy-start | bytes 3145732
  111.0 25.2 %copy-start.14 = (s32[32]{0:T(128)S(1)}, s32[32]{0:T(128)}, u32[]{:S(2)}) copy-start(s32[32]{0:T(128)} %get-tuple-element.8.pos_ref) | copy-start | bytes 388
  140.5 1.0 copy-start.6
  141.5 1.0 copy-start.8
  142.6 0.9 copy-start.10
  143.5 0.9 copy-start.11
  (2 other events, 1.6 us)
Sparse Core Ops, SparseCore 0:
  10.1 45.2 all-gather.1
  58.2 44.2 reduce-scatter.1
